TPU v7x, 128 devices: a whole 4x4x4 slice. The times are simulated.
128 devices in a mesh: comp: 8 (over z_lo, x), lon: 16 (over y, z_hi, core).
Axes of the slice: x: 4, y: 4, z: 4 (z_hi: 2, z_lo: 2; z = z_hi * 2 + z_lo), core: 2. Of those that a mesh axis runs over, the one named last changes fastest.
Arguments:
- fluxes: bfloat16 [10, 128, 12288], P(None, ('comp', 'lon')), may hold values from -6 to 6
- tracers: float32 [3, 40, 128, 10240], P(None, None, 'comp', 'lon'), may hold values from -6 to 6
- diffusivity: float32 [40, 128, 10240], P(None, 'comp', 'lon'), may hold values from 0.01 to 0.05
- east_speed: float32 [40, 128, 10240], P(None, 'comp', 'lon'), may hold values from -0.2 to 0.2
- north_speed: float32 [40, 128, 10240], P(None, 'comp', 'lon'), may hold values from -0.2 to 0.2
- wet: int32 [128, 10240], P('comp', 'lon'), may hold values 0 or 1
- coupling: float32 [3, 10], replicated, may hold values from -2 to 2
- sources: int32 [10240, 4], P(('comp', 'lon')), may hold values from 0 to 95, as said below
- live_slots: int32 [10240], P(('comp', 'lon')), may hold values from 1 to 4, as said below
- tiles: bfloat16 [10240, 4, 128, 128], P(('comp', 'lon')), may hold values from -0.25 to 0.25
Outputs:
- ocean: float32 [3, 40, 128, 10240], P(None, None, 'comp', 'lon')
Inputs may be any that keep to these rules, and one draw needn't show every extreme that they name: `sources`: a source block of the atmosphere rows of the target's comp band within the target's lon block. Slots k < live_slots[t] count, the others are padding.
All inputs are finite; a program needn't handle non-finite values. No bound on the sum of `wet` on one device may be relied on, other than what follows from the above.
Results may differ from a plain program's by a relative error of at most 0.009.
Values may be sent and summed in bfloat16 or wider, within the bound.
No kernel may reach another device: no remote copies, remote signals or barrier semaphores. Data moves between devices by JAX's collectives and lax.ppermute only.
A program may use at most 192 MiB of HBM per device.

v0:
```python
import functools

import jax
import jax.numpy as jnp
from jax import lax
from jax.experimental import pallas as pl
from jax.experimental.pallas import tpu as pltpu
from jax.sharding import PartitionSpec as P

VMIX = 0.2
L = 128
F32 = jnp.float32
BF = jnp.bfloat16
ANY = pl.BlockSpec(memory_space=pltpu.HBM)
VM = pl.BlockSpec(memory_space=pltpu.VMEM)
SM = pl.BlockSpec(memory_space=pltpu.SMEM)
NB, NR, NZ, NY = 5, 3, 40, 16
NQ = NR * NZ
ZP = NZ + 2


def lanes(rows=NY):
    return lax.broadcasted_iota(jnp.int32, (rows, L), 1)


def subl(rows=NY):
    return lax.broadcasted_iota(jnp.int32, (rows, L), 0)


def col(b):
    return slice(b * L, (b + 1) * L)


def east_of(vals, rows=8):
    rolled = [pltpu.roll(v, L - 1, 1) for v in vals]
    last = lanes(rows) == L - 1
    return [jnp.where(last, rolled[b + 1], rolled[b]) if b < NB - 1 else rolled[b] for b in range(NB)]


def west_of(vals, rows=8):
    rolled = [pltpu.roll(v, 1, 1) for v in vals]
    head = lanes(rows) == 0
    return [jnp.where(head, rolled[b - 1], rolled[b]) if b else rolled[b] for b in range(NB)]


def every2(flat, at):
    return flat[pl.ds(at, 8, stride=2), :]


def bcast(ref, b, j):
    return jnp.broadcast_to(ref[b, pl.ds(j, 1), :], (8, L))


def pack_ns_kernel(idx, q_h, k_h, n_h, wet_h, ns1, ns2, q_v, k_v, n_v, wet_i, rows_n, rows_s, sem):
    cw = pltpu.make_async_copy(wet_h, wet_i, sem.at[0])
    cw.start()
    copies = []
    for b in range(NB):
        at = pl.ds(b * L, L)
        copies.append(pltpu.make_async_copy(q_h.at[:, :, :, at], q_v.at[b], sem.at[1 + 3 * b]))
        copies.append(pltpu.make_async_copy(k_h.at[:, :, at], k_v.at[b], sem.at[2 + 3 * b]))
        copies.append(pltpu.make_async_copy(n_h.at[:, :, at], n_v.at[b], sem.at[3 + 3 * b]))
    for cp in copies:
        cp.start()
    cw.wait()
    even = idx[0] == 1
    for b in range(NB):
        for cp in copies[3 * b : 3 * b + 3]:
            cp.wait()
        for ref, count, base in ((q_v, NQ, 0), (k_v, NZ, NQ), (n_v, NZ, NQ + NZ)):
            flat = ref.reshape(NB * count * NY, L)
            for g in range(0, count, 8):
                at = (b * count + g) * NY
                rows_n[base + g : base + g + 8, :] = flat[pl.ds(at + NY - 1, 8, stride=NY), :]
                rows_s[base + g : base + g + 8, :] = flat[pl.ds(at, 8, stride=NY), :]
        w = wet_i[:, col(b)].astype(F32)
        rows_n[200:208, :] = jnp.broadcast_to(w[NY - 1 : NY, :], (8, L))
        rows_s[200:208, :] = jnp.broadcast_to(w[0:1, :], (8, L))
        for g in range(0, 208, 16):
            n, s = rows_n[g : g + 16, :], rows_s[g : g + 16, :]
            ns1[b, g : g + 16, :] = jnp.where(even, n, s).astype(BF)
            ns2[b, g : g + 16, :] = jnp.where(even, s, n).astype(BF)


def pack_lon_kernel(idx, flux_h, q_h, k_h, e_h, wet_h, after, a2a, hown, flux, q_v, k_v, e_v, wet_i, sem):
    pairs = [
        (flux_h, flux), (wet_h, wet_i),
        (q_h.at[:, :, :, pl.ds(4 * L, L)], q_v.at[1]), (q_h.at[:, :, :, pl.ds(0, L)], q_v.at[0]),
        (k_h.at[:, :, pl.ds(4 * L, L)], k_v.at[1]), (k_h.at[:, :, pl.ds(0, L)], k_v.at[0]),
        (e_h.at[:, :, pl.ds(4 * L, L)], e_v),
    ]
    copies = [pltpu.make_async_copy(a, b, sem.at[n]) for n, (a, b) in enumerate(pairs)]
    for cp in copies:
        cp.start()
    copies[0].wait()
    pad = jnp.zeros((6, L), BF)
    for d in range(16):
        for m in range(6):
            a2a[d, m] = jnp.concatenate([flux[:, col(d * 6 + m)], pad], axis=0)
    for cp in copies[1:]:
        cp.wait()
    lane = lanes()
    zero = jnp.zeros((NY, L), F32)

    def edge(z, carry):
        e0, e1, w0, w1 = carry
        for r in range(NR):
            j = r * NZ + z
            here = lane == j
            e0 = jnp.where(here, pltpu.roll(q_v[1, r, z], j + 1, 1), e0)
            w0 = jnp.where(here, pltpu.roll(q_v[0, r, z], j, 1), w0)
        here = lane == z
        e1 = jnp.where(here, pltpu.roll(k_v[1, z], z + 1, 1), e1)
        w1 = jnp.where(here, pltpu.roll(k_v[0, z], z, 1), w1)
        e1 = jnp.where(lane == z + NZ, pltpu.roll(e_v[z], z + NZ + 1, 1), e1)
        return e0, e1, w0, w1

    e0, e1, w0, w1 = lax.fori_loop(0, NZ, edge, (zero, zero, zero, zero), unroll=4)
    e0 = jnp.where(lane == NQ, pltpu.roll(wet_i[:, col(4)].astype(F32), NQ + 1, 1), e0)
    w0 = jnp.where(lane == NQ, pltpu.roll(wet_i[:, col(0)].astype(F32), NQ, 1), w0)
    hown[0], hown[1], hown[2], hown[3] = e0, e1, w0, w1
    l_east, l_west = idx[2], idx[3]
    a2a[l_east, 6] = e0.astype(BF)
    a2a[l_east, 7] = e1.astype(BF)
    a2a[l_west, 6] = w0.astype(BF)
    a2a[l_west, 7] = w1.astype(BF)


def stencil(flat, coef, z, halo_n, halo_s, vv, put):
    zu, zd = jnp.maximum(z - 1, 0), jnp.minimum(z + 1, NZ - 1)
    c0, ce, cw, cn, cs = coef
    sub = subl(8)
    for r in range(NR):
        def at(b, zz):
            return pl.multiple_of(((b * NR + r) * ZP + zz + 1) * NY, NY)

        ev = [every2(flat, at(b, z)) for b in range(NB)]
        od = [every2(flat, at(b, z) + 1) for b in range(NB)]
        east = [east_of(ev), east_of(od)]
        west = [west_of(ev), west_of(od)]
        j = r * NZ + z
        for b in range(NB):
            north_od = jnp.where(sub == 7, bcast(halo_n, b, j), every2(flat, at(b, z) + 2))
            south_ev = jnp.where(sub == 0, bcast(halo_s, b, j), every2(flat, at(b, z) - 1))
            north, south = (od[b], north_od), (south_ev, ev[b])
            outs = []
            for h, q in enumerate((ev[b], od[b])):
                out = c0[b][h] * q + ce[b][h] * east[h][b] + cw[b][h] * west[h][b]
                out = out + cn[b][h] * north[h] + cs[b][h] * south[h]
                outs.append(out + vv[b][h] * (every2(flat, at(b, zu) + h) + every2(flat, at(b, zd) + h)))
            put(b, r, j, outs)


CH = 8


def step1_kernel(
    idx, r1, r2, wet_h, q_h, k_h, e_h, n_h,
    first, coefs, rows, cols,
    q_v, k_v, e_v, n_v, f_v, c_v, wet_i, w_v, hn, hs, pe, pn, an0, bn0, sem, osem,
):
    cw = pltpu.make_async_copy(wet_h, wet_i, sem.at[NZ // CH, 0])
    cw.start()

    def fetch(i):
        out, z0 = [], i * CH
        zs = pl.ds(z0, CH)
        for b in range(NB):
            at = pl.ds(b * L, L)
            out.append(pltpu.make_async_copy(q_h.at[:, zs, :, at], q_v.at[b, :, pl.ds(z0 + 1, CH)], sem.at[i, 4 * b]))
            out.append(pltpu.make_async_copy(k_h.at[zs, :, at], k_v.at[b, pl.ds(z0 + 1, CH)], sem.at[i, 4 * b + 1]))
            out.append(pltpu.make_async_copy(e_h.at[zs, :, at], e_v.at[b, zs], sem.at[i, 4 * b + 2]))
            out.append(pltpu.make_async_copy(n_h.at[zs, :, at], n_v.at[b, zs], sem.at[i, 4 * b + 3]))
        return out

    def store(i):
        z0 = i * CH
        return [
            pltpu.make_async_copy(f_v.at[:, :, pl.ds(z0, CH)], first.at[:, :, pl.ds(z0 + 1, CH)], osem.at[i, 0]),
            pltpu.make_async_copy(c_v.at[:, :, pl.ds(z0, CH)], coefs.at[:, :, pl.ds(z0, CH)], osem.at[i, 1]),
        ]

    for i in range(NZ // CH):
        for cp in fetch(i):
            cp.start()
    even = idx[0] == 1
    for g in range(0, 208, 16):
        a, c = r1[:, g : g + 16, :].astype(F32), r2[:, g : g + 16, :].astype(F32)
        hn[:, g : g + 16, :] = jnp.where(even, a, c)
        hs[:, g : g + 16, :] = jnp.where(even, c, a)
    cw.wait()
    for b in range(NB):
        w_v[b] = wet_i[:, col(b)].astype(F32)
    wflat = w_v.reshape(NB * NY, L)
    w = [[every2(wflat, b * NY + h) for b in range(NB)] for h in range(2)]
    sub, lane = subl(8), lanes(8)
    we = [east_of(w[0]), east_of(w[1])]
    for b in range(NB):
        hw = jnp.broadcast_to(hn[b, 200:201, :], (8, L))
        wn = (w[1][b], jnp.where(sub == 7, hw, pltpu.roll(w[0][b], 7, 0)))
        for h in range(2):
            p = w[h][b] * we[h][b]
            pe[b, h] = jnp.where(lane == L - 1, 0.0, p) if b == NB - 1 else p
            pn[b, h] = w[h][b] * wn[h]
    for cp in fetch(0):
        cp.wait()

    def level(z, carry):
        he, hw = carry
        kflat = k_v.reshape(NB * ZP * NY, L)
        eflat, nflat = e_v.reshape(NB * NZ * NY, L), n_v.reshape(NB * NZ * NY, L)
        ks, ns = [[], []], [[], []]
        ae, be = [[], []], [[], []]
        for b in range(NB):
            at = pl.multiple_of((b * ZP + z + 1) * NY, NY)
            for h in range(2):
                ks[h].append(every2(kflat, at + h))
        for h in range(2):
            ke = east_of(ks[h])
            for b in range(NB):
                at = pl.multiple_of((b * NZ + z) * NY, NY)
                d = 0.5 * (ks[h][b] + ke[b]) * pe[b, h]
                u = every2(eflat, at + h) * pe[b, h]
                ae[h].append(jnp.maximum(u, 0.0) + d)
                be[h].append(jnp.minimum(u, 0.0) - d)
        aw, bw = [west_of(ae[0]), west_of(ae[1])], [west_of(be[0]), west_of(be[1])]
        coef = [[], [], [], [], []]
        vv = []
        for b in range(NB):
            at = pl.multiple_of((b * ZP + z + 1) * NY, NY)
            kn = (ks[1][b], jnp.where(sub == 7, bcast(hn, b, NQ + z), every2(kflat, at + 2)))
            at = pl.multiple_of((b * NZ + z) * NY, NY)
            an, bn = [], []
            for h in range(2):
                d = 0.5 * (ks[h][b] + kn[h]) * pn[b, h]
                u = every2(nflat, at + h) * pn[b, h]
                an.append(jnp.maximum(u, 0.0) + d)
                bn.append(jnp.minimum(u, 0.0) - d)
            ps = bcast(hs, b, 200) * jnp.broadcast_to(w_v[b, 0:1, :], (8, L))
            d = 0.5 * (bcast(hs, b, NQ + z) + jnp.broadcast_to(ks[0][b][0:1, :], (8, L))) * ps
            u = bcast(hs, b, NQ + NZ + z) * ps
            a_s = (jnp.where(sub == 0, jnp.maximum(u, 0.0) + d, pltpu.roll(an[1], 1, 0)), an[0])
            b_s = (jnp.where(sub == 0, jnp.minimum(u, 0.0) - d, pltpu.roll(bn[1], 1, 0)), bn[0])
            v = [VMIX * every2(wflat, b * NY + h) for h in range(2)]
            vals = []
            for h in range(2):
                a_w, b_w = aw[h][b], bw[h][b]
                if b == 0:
                    a_w, b_w = jnp.where(lane == 0, 0.0, a_w), jnp.where(lane == 0, 0.0, b_w)
                c0 = 1.0 - ae[h][b] + b_w - an[h] + b_s[h] - 2.0 * v[h]
                vals.append((c0, -be[h][b], a_w, -bn[h], a_s[h]))
                for n in range(5):
                    c_v[n, b, z, h] = vals[h][n]
            for n in range(5):
                coef[n].append((vals[0][n], vals[1][n]))
            vv.append(v)
        out = [he, hw]

        def put(b, r, j, outs):
            ff = f_v.reshape(NB * NQ * NY, L)
            at = pl.multiple_of((b * NQ + j) * NY, NY)
            for h in range(2):
                ff[pl.ds(at + h, 8, stride=2), :] = outs[h]
            if b == 0:
                out[1] = tuple(jnp.where(lane == j, pltpu.roll(outs[h], j, 1), out[1][h]) for h in range(2))
            if b == NB - 1:
                out[0] = tuple(jnp.where(lane == j, pltpu.roll(outs[h], j + 1, 1), out[0][h]) for h in range(2))

        stencil(q_v.reshape(NB * NR * ZP * NY, L), coef, z, hn, hs, vv, put)
        return tuple(out)

    zero = jnp.zeros((8, L), F32)
    carry = ((zero, zero), (zero, zero))

    def chunk(i, carry):
        carry = lax.fori_loop(i * CH, (i + 1) * CH - 1, level, carry)

        @pl.when(i < NZ // CH - 1)
        def _():
            for cp in fetch(jnp.minimum(i + 1, NZ // CH - 1)):
                cp.wait()

        carry = level((i + 1) * CH - 1, carry)
        for cp in store(i):
            cp.start()
        return carry

    he, hw = lax.fori_loop(0, NZ // CH, chunk, carry)
    cflat = cols.reshape(2 * NY, L)
    for h in range(2):
        cflat[pl.ds(h, 8, stride=2), :] = he[h]
        cflat[pl.ds(NY + h, 8, stride=2), :] = hw[h]
    ff = f_v.reshape(NB * NQ * NY, L)
    for b in range(NB):
        for g in range(0, NQ, 8):
            at = (b * NQ + g) * NY
            rows[0, b, g : g + 8, :] = ff[pl.ds(at + NY - 1, 8, stride=NY), :]
            rows[1, b, g : g + 8, :] = ff[pl.ds(at, 8, stride=NY), :]
    for i in range(NZ // CH):
        for cp in store(i):
            cp.wait()


def spread3(x):
    x = jnp.where(lanes() < NZ, x, 0.0)
    return x + pltpu.roll(x, NZ, 1) + pltpu.roll(x, 2 * NZ, 1)


def face(w_a, w_b, k_a, k_b, u):
    p = w_a * w_b
    d = 0.5 * (k_a + k_b) * p
    s = u * p
    return spread3(jnp.maximum(s, 0.0) + d), spread3(jnp.minimum(s, 0.0) - d)


def remap_kernel(
    idx, src, live, coup, got, tiles, wet, hown, rows, cols,
    forcing, ns1, ns2, ew1, ew2, hnew, facec, fluxes1,
):
    row = subl()
    zero = jnp.zeros((NY, L), F32)
    cvec = []
    for r in range(NR):
        c = zero
        for f in range(10):
            c = jnp.where(row == f, coup[r, f], c)
        cvec.append(c)

    def target_row(i, _):
        for s in range(NB):
            t = i * NB + s
            n = live[t]
            parts = []
            for k in range(4):
                p = src[k, t]
                blk = got[p // 6 * 8 + p % 6]
                parts.append(jnp.where(k < n, blk, jnp.zeros_like(blk)))
            acc = jnp.dot(jnp.concatenate(parts, axis=1), tiles[t], preferred_element_type=F32)
            for r in range(NR):
                forcing[s, r, pl.ds(i, 1), :] = jnp.sum(acc * cvec[r], axis=0, keepdims=True)
        return 0

    lax.fori_loop(0, NY, target_row, 0, unroll=2)
    for s in range(NB):
        w = wet[:, col(s)].astype(F32)
        for r in range(NR):
            forcing[s, r] = forcing[s, r] * w
    l_east, l_west = idx[2], idx[3]
    oe0, oe1, ow0, ow1 = hown[0], hown[1], hown[2], hown[3]
    ge0, ge1 = got[l_east * 8 + 6].astype(F32), got[l_east * 8 + 7].astype(F32)
    gw0, gw1 = got[l_west * 8 + 6].astype(F32), got[l_west * 8 + 7].astype(F32)

    def wcol(x):
        return jnp.broadcast_to(x[:, NQ : NQ + 1], (NY, L))

    ae, be = face(wcol(oe0), wcol(ge0), oe1, ge1, pltpu.roll(oe1, L - NZ, 1))
    aw, bw = face(wcol(gw0), wcol(ow0), gw1, ow1, pltpu.roll(gw1, L - NZ, 1))
    facec[0], facec[1], facec[2], facec[3] = ae, be, aw, bw
    fe = ae * oe0 + be * ge0
    fw = aw * gw0 + bw * ow0
    fluxes1[0], fluxes1[1] = fe, fw
    lane = lanes()
    he, hw = cols[0] - fe, cols[1] + fw
    for r in range(NR):
        here = lane == r * NZ
        he = he + jnp.where(here, pltpu.roll(forcing[4, r], r * NZ + 1, 1), 0.0)
        hw = hw + jnp.where(here, pltpu.roll(forcing[0, r], r * NZ, 1), 0.0)
    hnew[0], hnew[1] = he, hw
    leven = idx[1] == 1
    ew1[...] = jnp.where(leven, he, hw).astype(BF)
    ew2[...] = jnp.where(leven, hw, he).astype(BF)
    fill = jnp.zeros((L - NY, L), F32)
    fet = jnp.concatenate([fe, fill], axis=0).T
    fwt = jnp.concatenate([fw, fill], axis=0).T
    even = idx[0] == 1
    big = lanes(L)
    sub = subl(L)
    for b in range(NB):
        edges = []
        for side, y in ((0, NY - 1), (1, 0)):
            v = rows[side, b]
            for r in range(NR):
                v = v + jnp.where(sub == r * NZ, jnp.broadcast_to(forcing[b, r, y : y + 1, :], (L, L)), 0.0)
            if b == NB - 1:
                v = v - jnp.where(big == L - 1, jnp.broadcast_to(fet[:, y : y + 1], (L, L)), 0.0)
            if b == 0:
                v = v + jnp.where(big == 0, jnp.broadcast_to(fwt[:, y : y + 1], (L, L)), 0.0)
            edges.append(v)
        n, s = edges
        ns1[b] = jnp.where(even, n, s).astype(BF)
        ns2[b] = jnp.where(even, s, n).astype(BF)


def step2_kernel(
    idx, r1, r2, g1, g2, wet, forcing, hnew, facec, fluxes1, first_in, coefs,
    first, out_h,
    hn, hs, out_v, dl, w_v, sem,
):
    even = idx[0] == 1
    for g in range(0, 128, 16):
        a, c = r1[:, g : g + 16, :].astype(F32), r2[:, g : g + 16, :].astype(F32)
        hn[:, g : g + 16, :] = jnp.where(even, a, c)
        hs[:, g : g + 16, :] = jnp.where(even, c, a)
    leven = idx[1] == 1
    a, c = g1[...].astype(F32), g2[...].astype(F32)
    from_e, from_w = jnp.where(leven, a, c), jnp.where(leven, c, a)
    dl[0] = facec[0] * hnew[0] + facec[1] * from_e
    dl[1] = facec[2] * from_w + facec[3] * hnew[1]
    for b in range(NB):
        w_v[b] = wet[:, col(b)].astype(F32)
    wflat, dflat = w_v.reshape(NB * NY, L), dl.reshape(2 * NY, L)
    lane = lanes()

    def fix(z, _):
        for r in range(NR):
            j = r * NZ + z
            first[4, r, z + 1] = first_in[4, r, z + 1] - jnp.where(
                lane == L - 1, pltpu.roll(fluxes1[0], L - 1 - j, 1), 0.0
            )
            first[0, r, z + 1] = first_in[0, r, z + 1] + jnp.where(lane == 0, pltpu.roll(fluxes1[1], L - j, 1), 0.0)
        return 0

    lax.fori_loop(0, NZ, fix, 0, unroll=4)
    for b in range(NB):
        for r in range(NR):
            first[b, r, 1] = first[b, r, 1] + forcing[b, r]
    lane8 = lanes(8)

    def copy(i, b):
        z0 = i * CH
        return pltpu.make_async_copy(
            out_v.at[b, :, pl.ds(z0, CH)], out_h.at[:, pl.ds(z0, CH), :, pl.ds(b * L, L)], sem.at[i, b]
        )

    def level(z, _):
        coef = [[(coefs[n, b, z, 0], coefs[n, b, z, 1]) for b in range(NB)] for n in range(5)]
        vv = [[VMIX * every2(wflat, b * NY + h) for h in range(2)] for b in range(NB)]

        def put(b, r, j, outs):
            of = out_v.reshape(NB * NQ * NY, L)
            at = pl.multiple_of((b * NQ + j) * NY, NY)
            for h in range(2):
                o = outs[h]
                if b == 0:
                    o = o + jnp.where(lane8 == 0, pltpu.roll(every2(dflat, NY + h), L - j, 1), 0.0)
                if b == NB - 1:
                    o = o - jnp.where(lane8 == L - 1, pltpu.roll(every2(dflat, h), L - 1 - j, 1), 0.0)
                of[pl.ds(at + h, 8, stride=2), :] = o

        stencil(first.reshape(NB * NR * ZP * NY, L), coef, z, hn, hs, vv, put)
        return 0

    def chunk(i, _):
        lax.fori_loop(i * CH, (i + 1) * CH, level, 0)

        @pl.when(i == 0)
        def _():
            for b in range(NB):
                for r in range(NR):
                    out_v[b, r, 0] = out_v[b, r, 0] + forcing[b, r]

        for b in range(NB):
            copy(i, b).start()
        return 0

    lax.fori_loop(0, NZ // CH, chunk, 0)
    for i in range(NZ // CH):
        for b in range(NB):
            copy(i, b).wait()


def hbm(x):
    return pltpu.with_memory_space_constraint(x, pltpu.HBM)


def vmem(x):
    return pltpu.with_memory_space_constraint(x, pltpu.VMEM)


def shards(
    fluxes, tracers, diffusivity, east_speed, north_speed, wet, coupling, sources, live_slots, tiles
):
    sds = jax.ShapeDtypeStruct
    band, lon = lax.axis_index("comp"), lax.axis_index("lon")
    n_lon = lax.axis_size("lon")
    idx = jnp.stack([1 - band % 2, 1 - lon % 2, (lon + 1) % n_lon, (lon + n_lon - 1) % n_lon]).astype(jnp.int32)
    dma = pltpu.SemaphoreType.DMA
    q5, s5 = (NB, NR, NZ, NY, L), (NB, NZ, NY, L)
    qp, cf = (NB, NR, ZP, NY, L), (5, NB, NZ, 2, 8, L)
    rowpay, edgepay = (NB, 208, L), (NB, 128, L)

    def params(mib):
        return pltpu.CompilerParams(vmem_limit_bytes=mib << 20)

    flux, q, k, e, n, wh = map(
        hbm, (fluxes[:, 0, :], tracers, diffusivity, east_speed, north_speed, wet)
    )
    ns1, ns2 = pl.pallas_call(
        pack_ns_kernel,
        out_shape=(sds(rowpay, BF), sds(rowpay, BF)),
        in_specs=[SM] + [ANY] * 4,
        out_specs=(VM,) * 2,
        scratch_shapes=[
            pltpu.VMEM(q5, F32), pltpu.VMEM(s5, F32), pltpu.VMEM(s5, F32), pltpu.VMEM((NY, 640), jnp.int32),
            pltpu.VMEM((208, L), F32), pltpu.VMEM((208, L), F32), dma((16,)),
        ],
        compiler_params=params(16),
        name="pack_ns",
    )(idx, q, k, n, wh)
    swap_a = [(i, i ^ 1) for i in range(8)]
    swap_b = [(i, i + 1) for i in (1, 3, 5)] + [(i + 1, i) for i in (1, 3, 5)]
    r1 = lax.ppermute(ns1, "comp", swap_a)
    r2 = lax.ppermute(ns2, "comp", swap_b)
    a2a, hown = pl.pallas_call(
        pack_lon_kernel,
        out_shape=(sds((16, 8, NY, L), BF), sds((4, NY, L), F32)),
        in_specs=[SM] + [ANY] * 5 + [pl.BlockSpec(memory_space=pl.ANY)],
        out_specs=(VM,) * 2,
        scratch_shapes=[
            pltpu.VMEM((10, 12288), BF), pltpu.VMEM((2, NR, NZ, NY, L), F32), pltpu.VMEM((2, NZ, NY, L), F32),
            pltpu.VMEM((NZ, NY, L), F32), pltpu.VMEM((NY, 640), jnp.int32), dma((7,)),
        ],
        compiler_params=params(12),
        name="pack_lon",
    )(idx, flux, q, k, e, wh, ns1)
    got = lax.all_to_all(a2a, "lon", split_axis=0, concat_axis=0, tiled=True)
    first, coefs, rows, cols = pl.pallas_call(
        step1_kernel,
        out_shape=(sds(qp, F32), sds(cf, F32), sds((2,) + edgepay, F32), sds((2, NY, L), F32)),
        in_specs=[SM] + [VM] * 2 + [ANY] * 5,
        out_specs=(pl.BlockSpec(memory_space=pl.ANY),) * 2 + (VM,) * 2,
        scratch_shapes=[
            pltpu.VMEM(qp, F32), pltpu.VMEM((NB, ZP, NY, L), F32), pltpu.VMEM(s5, F32), pltpu.VMEM(s5, F32),
            pltpu.VMEM(q5, F32), pltpu.VMEM(cf, F32), pltpu.VMEM((NY, 640), jnp.int32), pltpu.VMEM((NB, NY, L), F32),
            pltpu.VMEM(rowpay, F32), pltpu.VMEM(rowpay, F32),
            pltpu.VMEM((NB, 2, 8, L), F32), pltpu.VMEM((NB, 2, 8, L), F32),
            pltpu.VMEM((8, L), F32), pltpu.VMEM((8, L), F32),
            dma((NZ // CH + 1, 4 * NB)), dma((NZ // CH, 2)),
        ],
        compiler_params=params(32),
        name="step1",
    )(idx, r1, r2, wh, q, k, e, n)
    forcing, ms1, ms2, ew1, ew2, hnew, facec, fluxes1 = pl.pallas_call(
        remap_kernel,
        out_shape=(
            sds((NB, NR, NY, L), F32), sds(edgepay, BF), sds(edgepay, BF), sds((NY, L), BF), sds((NY, L), BF),
            sds((2, NY, L), F32), sds((4, NY, L), F32), sds((2, NY, L), F32),
        ),
        in_specs=[SM] * 4 + [VM] * 6,
        out_specs=(VM,) * 8,
        compiler_params=params(6),
        name="remap",
    )(idx, sources.T, live_slots, coupling, got.reshape(128, NY, L), vmem(tiles.reshape(80, 512, L)), wet, hown, rows, cols)
    lon_a = [(i, i ^ 1) for i in range(16)]
    lon_b = [((2 * i + 1) % 16, (2 * i + 2) % 16) for i in range(8)]
    lon_b = lon_b + [(b, a) for a, b in lon_b]
    r1 = lax.ppermute(ms1, "comp", swap_a)
    r2 = lax.ppermute(ms2, "comp", swap_b)
    g1 = lax.ppermute(ew1, "lon", lon_a)
    g2 = lax.ppermute(ew2, "lon", lon_b)
    return pl.pallas_call(
        step2_kernel,
        out_shape=(pltpu.VMEM(qp, F32), sds(tracers.shape, F32)),
        in_specs=[SM] + [VM] * 11,
        out_specs=(VM, ANY),
        scratch_shapes=[
            pltpu.VMEM(edgepay, F32), pltpu.VMEM(edgepay, F32), pltpu.VMEM(q5, F32),
            pltpu.VMEM((2, NY, L), F32), pltpu.VMEM((NB, NY, L), F32), dma((NZ // CH, NB)),
        ],
        input_output_aliases={10: 0},
        compiler_params=params(10),
        name="step2",
    )(idx, r1, r2, g1, g2, wet, forcing, hnew, facec, fluxes1, vmem(first), vmem(coefs))[1]


def solution(mesh):
    return jax.shard_map(
        shards,
        mesh=mesh,
        in_specs=(
            P(None, ("comp", "lon"), None),
            P(None, None, "comp", "lon"),
            P(None, "comp", "lon"),
            P(None, "comp", "lon"),
            P(None, "comp", "lon"),
            P("comp", "lon"),
            P(),
            P(("comp", "lon"), None),
            P(("comp", "lon")),
            P(("comp", "lon"), None, None, None),
        ),
        out_specs=P(None, None, "comp", "lon"),
        check_vma=False,
    )
```

profile of v0, /device:TPU:2, one launch (start us, length us, event | category | flops | bytes accessed | tf_op | source)
XLA Modules:
  0.0 86.8 jit_solution(3241245892289175309)
XLA Ops:
  0.0 0.1 pad_add_fusion.idx
  0.1 4.2 %pack_ns.1 = (bf16[5,208,128]{2,1,0:T(8,128)(2,1)S(1)}, bf16[5,208,128]{2,1,0:T(8,128)(2,1)S(1)}) custom-call(s32[4]{0:T(128)S(1)} %pad_add_fusion.idx, f32[3,40,16,640]{3,2,1,0:T(8,128)} %q_h.5, f32[40,16,640]{2,1,0:T(8,128)} %k_h.5, f32[40,16,640]{2,1,0:T(8,128)} %n_h.3, s32[16,640]{1,0:T(8,128)} %wet.3), custom_call_target="tpu_custom_call" | custom-call | tf_op jit(solution)/shard_map/pack_ns/pallas_call | solution.py:498
  4.3 4.8 %pack_lon.1 = (bf16[16,8,16,128]{3,2,1,0:T(8,128)(2,1)}, f32[4,16,128]{2,1,0:T(8,128)S(1)}) custom-call(s32[4]{0:T(128)S(1)} %pad_add_fusion.idx, bf16[10,12288]{1,0:T(8,128)(2,1)} %bitcast.11, f32[3,40,16,640]{3,2,1,0:T(8,128)} %q_h.5, f32[40,16,640]{2,1,0:T(8,128)} %k_h.5, f32[40,16,640]{2,1,0:T(8,128)} %e_h.3, s32[16,640]{1,0:T(8,128)} %wet.3, ...), custom_call_target="tpu_custom_call" | custom-call | tf_op jit(solution)/shard_map/pack_lon/pallas_call | solution.py:514
  9.1 7.9 %all-to-all-start = ((bf16[16,8,16,128]{3,2,1,0:T(8,128)(2,1)}), bf16[16,8,16,128]{3,2,1,0:T(8,128)(2,1)S(1)}, u32[]{:S(2)}, u32[]{:S(2)}) async-start(bf16[16,8,16,128]{3,2,1,0:T(8,128)(2,1)} %get-tuple-element.23), calls=%async_computation | async-start | bytes 1048576 | tf_op jit(solution)/shard_map/all_to_all | solution.py:526
  17.0 0.0 copy-start.5
  17.0 0.0 copy-start.6
  17.1 0.0 copy-start.7
  17.1 3.5 %collective-permute-start.1 = (bf16[5,208,128]{2,1,0:T(8,128)(2,1)S(1)}, bf16[5,208,128]{2,1,0:T(8,128)(2,1)S(1)}, u32[]{:S(2)}, u32[]{:S(2)}) collective-permute-start(bf16[5,208,128]{2,1,0:T(8,128)(2,1)S(1)} %get-tuple-element.25), channel_id=1, source_target_pairs={{16,32},{48,64},{80,96},{32,16},{64,48},{96,80},{17,33},{49,65},{8... | collective-permute-start | bytes 798728 | tf_op jit(solution)/shard_map/ppermute | solution.py:513
  20.6 0.1 collective-permute-start
  20.7 7.1 %collective-permute-done.1.r2 = bf16[5,208,128]{2,1,0:T(8,128)(2,1)S(1)} collective-permute-done((bf16[5,208,128]{2,1,0:T(8,128)(2,1)S(1)}, bf16[5,208,128]{2,1,0:T(8,128)(2,1)S(1)}, u32[]{:S(2)}, u32[]{:S(2)}) %collective-permute-start.1) | collective-permute-done | bytes 266272 | tf_op jit(solution)/shard_map/ppermute | solution.py:513
  27.8 1.3 %collective-permute-done.r1 = bf16[5,208,128]{2,1,0:T(8,128)(2,1)S(1)} collective-permute-done((bf16[5,208,128]{2,1,0:T(8,128)(2,1)S(1)}, bf16[5,208,128]{2,1,0:T(8,128)(2,1)S(1)}, u32[]{:S(2)}, u32[]{:S(2)}) %collective-permute-start) | collective-permute-done | bytes 266272 | tf_op jit(solution)/shard_map/ppermute | solution.py:512
  29.1 15.8 %step1.1 = (f32[5,3,42,16,128]{4,3,2,1,0:T(8,128)S(1)}, f32[5,5,40,2,8,128]{5,4,3,2,1,0:T(8,128)S(1)}, f32[2,5,128,128]{3,2,1,0:T(8,128)S(1)}, f32[2,16,128]{2,1,0:T(8,128)S(1)}) custom-call(s32[4]{0:T(128)S(1)} %pad_add_fusion.idx, bf16[5,208,128]{2,1,0:T(8,128)(2,1)S(1)} %collective-permute-done.r1, bf16[5,208,128]{2,1,0:T(8,128)(2,1)S(1)} %collective-permute-done.1.r2, ...), custom_call_target="tpu_custom_call" | custom-call | tf_op jit(solution)/shard_map/step1/pallas_call | solution.py:527
  45.0 3.2 %copy-done.1 = f32[5,5,40,2,8,128]{5,4,3,2,1,0:T(8,128)} copy-done((f32[5,5,40,2,8,128]{5,4,3,2,1,0:T(8,128)}, f32[5,5,40,2,8,128]{5,4,3,2,1,0:T(8,128)S(1)}, u32[]{:S(2)}) %copy-start.1) | copy-done | bytes 8192024
  48.2 2.4 %copy-done.3 = f32[5,3,42,16,128]{4,3,2,1,0:T(8,128)} copy-done((f32[5,3,42,16,128]{4,3,2,1,0:T(8,128)}, f32[5,3,42,16,128]{4,3,2,1,0:T(8,128)S(1)}, u32[]{:S(2)}) %copy-start.3) | copy-done | bytes 5160984
  50.5 0.0 copy-start
  50.6 4.0 %copy-done = bf16[80,4,128,128]{3,2,1,0:T(8,128)(2,1)S(1)} copy-done((bf16[80,4,128,128]{3,2,1,0:T(8,128)(2,1)S(1)}, bf16[80,4,128,128]{3,2,1,0:T(8,128)(2,1)}, u32[]{:S(2)}) %copy-start) | copy-done | bytes 10485784
  54.5 4.7 %remap.1 = (f32[5,3,16,128]{3,2,1,0:T(8,128)S(1)}, bf16[5,128,128]{2,1,0:T(8,128)(2,1)S(1)}, bf16[5,128,128]{2,1,0:T(8,128)(2,1)S(1)}, bf16[16,128]{1,0:T(8,128)...) custom-call(s32[4]{0:T(128)S(1)} %pad_add_fusion.idx, ...), custom_call_target="tpu_custom_call" | custom-call | tf_op jit(solution)/shard_map/remap/pallas_call | solution.py:543
  59.2 0.4 collective-permute-start.2
  59.6 7.7 %collective-permute-start.3 = (bf16[5,128,128]{2,1,0:T(8,128)(2,1)S(1)}, bf16[5,128,128]{2,1,0:T(8,128)(2,1)S(1)}, u32[]{:S(2)}, u32[]{:S(2)}) collective-permute-start(bf16[5,128,128]{2,1,0:T(8,128)(2,1)S(1)} %get-tuple-element.29), channel_id=1, source_target_pairs={{16,32},{48,64},{80,96},{32,16},{64,48},{96,80},{17,33},{49,65},{8... | collective-permute-start | bytes 491528 | tf_op jit(solution)/shard_map/ppermute | solution.py:558
  67.3 0.1 collective-permute-start.4
  67.4 4.0 %collective-permute-start.5 = (bf16[16,128]{1,0:T(8,128)(2,1)S(1)}, bf16[16,128]{1,0:T(8,128)(2,1)S(1)}, u32[]{:S(2)}, u32[]{:S(2)}) collective-permute-start(bf16[16,128]{1,0:T(8,128)(2,1)S(1)} %get-tuple-element.31), channel_id=1, source_target_pairs={{1,2},{3,4},{5,6},{7,8},{9,10},{11,12},{13,14},{15,0},{2,1},{4,3},... | collective-permute-start | bytes 12296 | tf_op jit(solution)/shard_map/ppermute | solution.py:560
  71.4 2.7 %collective-permute-done.5.g2 = bf16[16,128]{1,0:T(8,128)(2,1)S(1)} collective-permute-done((bf16[16,128]{1,0:T(8,128)(2,1)S(1)}, bf16[16,128]{1,0:T(8,128)(2,1)S(1)}, u32[]{:S(2)}, u32[]{:S(2)}) %collective-permute-start.5) | collective-permute-done | bytes 4128 | tf_op jit(solution)/shard_map/ppermute | solution.py:560
  74.1 2.5 %copy-done.4 = f32[5,3,42,16,128]{4,3,2,1,0:T(8,128)S(1)} copy-done((f32[5,3,42,16,128]{4,3,2,1,0:T(8,128)S(1)}, f32[5,3,42,16,128]{4,3,2,1,0:T(8,128)}, u32[]{:S(2)}) %copy-start.4) | copy-done | bytes 5160984
  76.6 10.2 %step2.1 = (f32[5,3,42,16,128]{4,3,2,1,0:T(8,128)S(1)}, f32[3,40,16,640]{3,2,1,0:T(8,128)}) custom-call(s32[4]{0:T(128)S(1)} %pad_add_fusion.idx, bf16[5,128,128]{2,1,0:T(8,128)(2,1)S(1)} %collective-permute-done.2.r1, bf16[5,128,128]{2,1,0:T(8,128)(2,1)S(1)} %collective-permute-done.3.r2, ...), custom_call_target="tpu_custom_call", output_to_operand_aliasing={{0}: (10, {})} | custom-call | tf_op jit(solution)/shard_map/step2/pallas_call | solution.py:561
  (14 shorter events, 0.0 us)
Async XLA Ops:
  9.1 41.4 %all-to-all-start = ((bf16[16,8,16,128]{3,2,1,0:T(8,128)(2,1)}), bf16[16,8,16,128]{3,2,1,0:T(8,128)(2,1)S(1)}, u32[]{:S(2)}, u32[]{:S(2)}) async-start(bf16[16,8,16,128]{3,2,1,0:T(8,128)(2,1)} %get-tuple-element.23), calls=%async_computation | async-start | bytes 1048576 | tf_op jit(solution)/shard_map/all_to_all | solution.py:526
  17.0 33.5 %copy-start.5 = (s32[16,640]{1,0:T(8,128)S(1)}, s32[16,640]{1,0:T(8,128)}, u32[]{:S(2)}) copy-start(s32[16,640]{1,0:T(8,128)} %wet.3) | copy-start | bytes 122884
  17.0 33.5 %copy-start.6 = (s32[80,4]{0,1:T(4,128)S(1)}, s32[80,4]{0,1:T(4,128)}, u32[]{:S(2)}) copy-start(s32[80,4]{0,1:T(4,128)} %param.17) | copy-start | bytes 3844
  17.1 33.5 %copy-start.7 = (f32[3,10]{1,0:T(4,128)S(1)}, f32[3,10]{1,0:T(4,128)}, u32[]{:S(2)}) copy-start(f32[3,10]{1,0:T(4,128)} %coup.1) | copy-start | bytes 364
  17.1 33.5 %copy-start.8 = (s32[80]{0:T(128)S(1)}, s32[80]{0:T(128)}, u32[]{:S(2)}) copy-start(s32[80]{0:T(128)} %live.1) | copy-start | bytes 964
  17.1 10.8 %collective-permute-start.1 = (bf16[5,208,128]{2,1,0:T(8,128)(2,1)S(1)}, bf16[5,208,128]{2,1,0:T(8,128)(2,1)S(1)}, u32[]{:S(2)}, u32[]{:S(2)}) collective-permute-start(bf16[5,208,128]{2,1,0:T(8,128)(2,1)S(1)} %get-tuple-element.25), channel_id=1, source_target_pairs={{16,32},{48,64},{80,96},{32,16},{64,48},{96,80},{17,33},{49,65},{8... | collective-permute-start | bytes 798728 | tf_op jit(solution)/shard_map/ppermute | solution.py:513
  20.6 8.5 %collective-permute-start = (bf16[5,208,128]{2,1,0:T(8,128)(2,1)S(1)}, bf16[5,208,128]{2,1,0:T(8,128)(2,1)S(1)}, u32[]{:S(2)}, u32[]{:S(2)}) collective-permute-start(bf16[5,208,128]{2,1,0:T(8,128)(2,1)S(1)} %get-tuple-element.22.after), channel_id=1, source_target_pairs={{0,16},{16,0},{32,48},{48,32},{64,80},{80,64},{96,112},{112,96},{1... | collective-permute-start | bytes 798728 | tf_op jit(solution)/shard_map/ppermute | solution.py:512
  45.0 3.2 %copy-start.1 = (f32[5,5,40,2,8,128]{5,4,3,2,1,0:T(8,128)}, f32[5,5,40,2,8,128]{5,4,3,2,1,0:T(8,128)S(1)}, u32[]{:S(2)}) copy-start(f32[5,5,40,2,8,128]{5,4,3,2,1,0:T(8,128)S(1)} %get-tuple-element.37.coefs) | copy-start | bytes 24576004
  48.2 2.4 %copy-start.3 = (f32[5,3,42,16,128]{4,3,2,1,0:T(8,128)}, f32[5,3,42,16,128]{4,3,2,1,0:T(8,128)S(1)}, u32[]{:S(2)}) copy-start(f32[5,3,42,16,128]{4,3,2,1,0:T(8,128)S(1)} %get-tuple-element.36.first_in) | copy-start | bytes 15482884
  50.5 4.0 %copy-start = (bf16[80,4,128,128]{3,2,1,0:T(8,128)(2,1)S(1)}, bf16[80,4,128,128]{3,2,1,0:T(8,128)(2,1)}, u32[]{:S(2)}) copy-start(bf16[80,4,128,128]{3,2,1,0:T(8,128)(2,1)} %param.19) | copy-start | bytes 31457284
  54.5 19.6 %copy-start.2 = (f32[5,5,40,2,8,128]{5,4,3,2,1,0:T(8,128)S(1)}, f32[5,5,40,2,8,128]{5,4,3,2,1,0:T(8,128)}, u32[]{:S(2)}) copy-start(f32[5,5,40,2,8,128]{5,4,3,2,1,0:T(8,128)} %copy-done.1) | copy-start | bytes 24576004
  59.2 14.9 %collective-permute-start.2 = (bf16[5,128,128]{2,1,0:T(8,128)(2,1)S(1)}, bf16[5,128,128]{2,1,0:T(8,128)(2,1)S(1)}, u32[]{:S(2)}, u32[]{:S(2)}) collective-permute-start(bf16[5,128,128]{2,1,0:T(8,128)(2,1)S(1)} %get-tuple-element.28), channel_id=1, source_target_pairs={{0,16},{16,0},{32,48},{48,32},{64,80},{80,64},{96,112},{112,96},{1... | collective-permute-start | bytes 491528 | tf_op jit(solution)/shard_map/ppermute | solution.py:557
  59.6 14.5 %collective-permute-start.3 = (bf16[5,128,128]{2,1,0:T(8,128)(2,1)S(1)}, bf16[5,128,128]{2,1,0:T(8,128)(2,1)S(1)}, u32[]{:S(2)}, u32[]{:S(2)}) collective-permute-start(bf16[5,128,128]{2,1,0:T(8,128)(2,1)S(1)} %get-tuple-element.29), channel_id=1, source_target_pairs={{16,32},{48,64},{80,96},{32,16},{64,48},{96,80},{17,33},{49,65},{8... | collective-permute-start | bytes 491528 | tf_op jit(solution)/shard_map/ppermute | solution.py:558
  67.3 4.1 %collective-permute-start.4 = (bf16[16,128]{1,0:T(8,128)(2,1)S(1)}, bf16[16,128]{1,0:T(8,128)(2,1)S(1)}, u32[]{:S(2)}, u32[]{:S(2)}) collective-permute-start(bf16[16,128]{1,0:T(8,128)(2,1)S(1)} %get-tuple-element.30), channel_id=1, source_target_pairs={{0,1},{1,0},{2,3},{3,2},{4,5},{5,4},{6,7},{7,6},{8,9},{9,8},{10,11... | collective-permute-start | bytes 12296 | tf_op jit(solution)/shard_map/ppermute | solution.py:559
  67.4 6.7 %collective-permute-start.5 = (bf16[16,128]{1,0:T(8,128)(2,1)S(1)}, bf16[16,128]{1,0:T(8,128)(2,1)S(1)}, u32[]{:S(2)}, u32[]{:S(2)}) collective-permute-start(bf16[16,128]{1,0:T(8,128)(2,1)S(1)} %get-tuple-element.31), channel_id=1, source_target_pairs={{1,2},{3,4},{5,6},{7,8},{9,10},{11,12},{13,14},{15,0},{2,1},{4,3},... | collective-permute-start | bytes 12296 | tf_op jit(solution)/shard_map/ppermute | solution.py:560
  74.1 2.5 %copy-start.4 = (f32[5,3,42,16,128]{4,3,2,1,0:T(8,128)S(1)}, f32[5,3,42,16,128]{4,3,2,1,0:T(8,128)}, u32[]{:S(2)}) copy-start(f32[5,3,42,16,128]{4,3,2,1,0:T(8,128)} %copy-done.3) | copy-start | bytes 15482884
where the time goes:
time: 87.1 us; the launch traced here: 86.8 us
  Pallas kernels  39.8 us (46%)
  starting transfers between devices  23.6 us (27%)
  local copies, waits for them, and re-layouts  12 us (14%)
  waiting for transfers between devices  11.2 us (13%)
    pallas_call x1, Pallas kernels, shards(): pl.pallas_call(step1_kernel, out_shape=(sds(qp, F32), sds(cf, F32), sds((...  15.8 us
    unnamed x18, local copies, waits for them, and re-layouts  12 us
    pallas_call x1, Pallas kernels, shards(): pl.pallas_call(step2_kernel, out_shape=(pltpu.VMEM(qp, F32), sds(tracers....  10.2 us
    all_to_all x1, starting transfers between devices, shards(): got = lax.all_to_all(a2a, 'lon', split_axis=0, concat_axis=0, tiled=True)  7.9 us
    ppermute x1, starting transfers between devices, shards(): r2 = lax.ppermute(ms2, 'comp', swap_b)  7.67 us
    ppermute x1, waiting for transfers between devices, shards(): r2 = lax.ppermute(ns2, 'comp', swap_b)  7.12 us
    pallas_call x1, Pallas kernels, shards(): pl.pallas_call(pack_lon_kernel, out_shape=(sds((16, 8, NY, L), BF), sds((...  4.84 us
    pallas_call x1, Pallas kernels, shards(): pl.pallas_call(remap_kernel, out_shape=(sds((NB, NR, NY, L), F32), sds(ed...  4.71 us
  transfers between devices with their start and end apart: 7, of which 3 were waited for; matrix products, arithmetic and copies ran while one was open for 0% of the time, Pallas kernels for 18%

commit v1 on v0

v1 whole, which is shorter than its diff:
```python
import functools

import jax
import jax.numpy as jnp
from jax import lax
from jax.experimental import pallas as pl
from jax.experimental.pallas import tpu as pltpu
from jax.sharding import PartitionSpec as P

VMIX = 0.2
L = 128
F32 = jnp.float32
BF = jnp.bfloat16
ANY = pl.BlockSpec(memory_space=pltpu.HBM)
VM = pl.BlockSpec(memory_space=pltpu.VMEM)
SM = pl.BlockSpec(memory_space=pltpu.SMEM)
NB, NR, NZ, NY = 5, 3, 40, 16
NQ = NR * NZ
CH = 8
NC = NZ // CH
UNROLL1 = 2


def lanes(rows=NY):
    return lax.broadcasted_iota(jnp.int32, (rows, L), 1)


def subl(rows=NY):
    return lax.broadcasted_iota(jnp.int32, (rows, L), 0)


def col(b):
    return slice(b * L, (b + 1) * L)


def east_of(vals):
    rolled = [pltpu.roll(v, L - 1, 1) for v in vals]
    last = lanes() == L - 1
    return [jnp.where(last, rolled[b + 1], rolled[b]) if b < NB - 1 else rolled[b] for b in range(NB)]


def west_of(vals, wrap=False):
    rolled = [pltpu.roll(v, 1, 1) for v in vals]
    head = lanes() == 0
    return [jnp.where(head, rolled[b - 1], rolled[b]) if b or wrap else rolled[b] for b in range(NB)]


def to_lane(acc, val, h, source):
    return jnp.where(lanes() == h, pltpu.roll(val, (h - source) % L, 1), acc)


def pack_kernel(
    idx, flux_h, q_h, k_h, e_h, n_h, wet_h,
    a2a, ns1, ns2, hown, edge_n, edge_s,
    flux, q_v, k_v, n_v, e_v, wet_i, sem,
):
    first_two = [pltpu.make_async_copy(flux_h, flux, sem.at[0]), pltpu.make_async_copy(wet_h, wet_i, sem.at[1])]
    last_e = pltpu.make_async_copy(e_h.at[:, :, pl.ds(4 * L, L)], e_v, sem.at[2])
    copies = {}
    for b in range(NB):
        at = pl.ds(b * L, L)
        copies[b] = [
            pltpu.make_async_copy(q_h.at[:, :, :, at], q_v.at[b], sem.at[3 + 3 * b]),
            pltpu.make_async_copy(k_h.at[:, :, at], k_v.at[b], sem.at[4 + 3 * b]),
            pltpu.make_async_copy(n_h.at[:, :, at], n_v.at[b], sem.at[5 + 3 * b]),
        ]
    for cp in first_two:
        cp.start()
    order = (4, 0, 1, 2, 3)
    for b in order:
        for cp in copies[b]:
            cp.start()
        if b == 4:
            last_e.start()
    for cp in first_two:
        cp.wait()
    pad = jnp.zeros((6, L), BF)
    for d in range(16):
        for m in range(6):
            a2a[d, m] = jnp.concatenate([flux[:, col(d * 6 + m)], pad], axis=0)
    for b in (4, 0):
        for cp in copies[b]:
            cp.wait()
    last_e.wait()
    lane = lanes()
    zero = jnp.zeros((NY, L), F32)

    def edge(i, carry):
        e0, e1, w0, w1 = carry
        acc = [zero] * 9
        for h in range(CH):
            z = i * CH + h
            for r in range(NR):
                acc[r] = to_lane(acc[r], q_v[4, r, z], h, L - 1)
                acc[3 + r] = to_lane(acc[3 + r], q_v[0, r, z], h, 0)
            acc[6] = to_lane(acc[6], k_v[4, z], h, L - 1)
            acc[7] = to_lane(acc[7], e_v[z], h, L - 1)
            acc[8] = to_lane(acc[8], k_v[0, z], h, 0)
        for r in range(NR):
            e0 = e0 + pltpu.roll(acc[r], r * NZ + i * CH, 1)
            w0 = w0 + pltpu.roll(acc[3 + r], r * NZ + i * CH, 1)
        e1 = e1 + pltpu.roll(acc[6], i * CH, 1) + pltpu.roll(acc[7], NZ + i * CH, 1)
        w1 = w1 + pltpu.roll(acc[8], i * CH, 1)
        return e0, e1, w0, w1

    e0, e1, w0, w1 = lax.fori_loop(0, NC, edge, (zero, zero, zero, zero))
    e0 = jnp.where(lane == NQ, pltpu.roll(wet_i[:, col(4)].astype(F32), NQ + 1, 1), e0)
    w0 = jnp.where(lane == NQ, pltpu.roll(wet_i[:, col(0)].astype(F32), NQ, 1), w0)
    hown[0], hown[1], hown[2], hown[3] = e0, e1, w0, w1
    l_east, l_west = idx[2], idx[3]
    a2a[l_east, 6] = e0.astype(BF)
    a2a[l_east, 7] = e1.astype(BF)
    a2a[l_west, 6] = w0.astype(BF)
    a2a[l_west, 7] = w1.astype(BF)
    even = idx[0] == 1
    for b in order:
        if b not in (4, 0):
            for cp in copies[b]:
                cp.wait()
        for ref, count, base in ((q_v, NQ, 0), (k_v, NZ, NQ), (n_v, NZ, NQ + NZ)):
            flat = ref.reshape(NB * count * NY, L)
            for g in range(0, count, 8):
                at = (b * count + g) * NY
                edge_n[b, base + g : base + g + 8, :] = flat[pl.ds(at + NY - 1, 8, stride=NY), :]
                edge_s[b, base + g : base + g + 8, :] = flat[pl.ds(at, 8, stride=NY), :]
        w = wet_i[:, col(b)].astype(F32)
        edge_n[b, 200:208, :] = jnp.broadcast_to(w[NY - 1 : NY, :], (8, L))
        edge_s[b, 200:208, :] = jnp.broadcast_to(w[0:1, :], (8, L))
        for g in range(0, 208, 16):
            n, s = edge_n[b, g : g + 16, :], edge_s[b, g : g + 16, :]
            ns1[b, g : g + 16, :] = jnp.where(even, n, s).astype(BF)
            ns2[b, g : g + 16, :] = jnp.where(even, s, n).astype(BF)


def stencil(get, coef, z, mix, put):
    zu, zd = jnp.maximum(z - 1, 0), jnp.minimum(z + 1, NZ - 1)
    c0, ce, cw, cn, cs = coef
    for r in range(NR):
        q = [get(b, r, z) for b in range(NB)]
        qe, qw = east_of(q), west_of(q)
        j = r * NZ + z
        for b in range(NB):
            qn, qs = pltpu.roll(q[b], NY - 1, 0), pltpu.roll(q[b], 1, 0)
            out = c0[b] * q[b] + ce[b] * qe[b] + cw[b] * qw[b] + cn[b] * qn + cs[b] * qs
            put(b, r, j, out + mix[b] * (get(b, r, zu) + get(b, r, zd)))


def from_sides(idx, r1, r2, at):
    even = idx[0] == 1
    a, c = r1[at].astype(F32), r2[at].astype(F32)
    return jnp.where(even, a, c), jnp.where(even, c, a)


def add_rows(val, south, north):
    sub = subl(8)
    low = val[0:8] + jnp.where(sub == 0, jnp.broadcast_to(south, (8, L)), 0.0)
    high = val[8:16] - jnp.where(sub == 7, jnp.broadcast_to(north, (8, L)), 0.0)
    return jnp.concatenate([low, high], axis=0)


def step1_kernel(
    wet_h, q_h, k_h, e_h, n_h,
    first_h, coefs_h, rows, cols,
    q_v, k_v, e_v, n_v, first, coefs, wet_i, pe, pn, keep, mix, sem, osem,
):
    cw = pltpu.make_async_copy(wet_h, wet_i, sem.at[NC, 0])
    cw.start()

    def fetch(i):
        zs = pl.ds(i * CH, CH)
        return [
            pltpu.make_async_copy(q_h.at[:, zs], q_v.at[:, zs], sem.at[i, 0]),
            pltpu.make_async_copy(k_h.at[zs], k_v.at[zs], sem.at[i, 1]),
            pltpu.make_async_copy(e_h.at[zs], e_v.at[zs], sem.at[i, 2]),
            pltpu.make_async_copy(n_h.at[zs], n_v.at[zs], sem.at[i, 3]),
        ]

    def store(i):
        zs = pl.ds(i * CH, CH)
        return [
            pltpu.make_async_copy(first.at[:, :, zs], first_h.at[:, :, zs], osem.at[i, 0]),
            pltpu.make_async_copy(coefs.at[:, :, zs], coefs_h.at[:, :, zs], osem.at[i, 1]),
        ]

    for i in range(NC):
        for cp in fetch(i):
            cp.start()
    cw.wait()
    row, lane = subl(), lanes()
    w = [wet_i[:, col(b)].astype(F32) for b in range(NB)]
    we = east_of(w)
    for b in range(NB):
        p = w[b] * we[b]
        pe[b] = 0.5 * (jnp.where(lane == L - 1, 0.0, p) if b == NB - 1 else p)
        pn[b] = 0.5 * w[b] * jnp.where(row == NY - 1, 0.0, pltpu.roll(w[b], NY - 1, 0))
        mix[b] = VMIX * w[b]
        keep[b] = 1.0 - 2.0 * VMIX * w[b]
    for cp in fetch(0):
        cp.wait()

    def level(z):
        k = [k_v[z, :, col(b)] for b in range(NB)]
        ke = east_of(k)
        ae, be, an, bn = [], [], [], []
        for b in range(NB):
            kn = pltpu.roll(k[b], NY - 1, 0)
            d = (k[b] + ke[b]) * pe[b]
            u = 2.0 * e_v[z, :, col(b)] * pe[b]
            ae.append(jnp.maximum(u, 0.0) + d)
            be.append(jnp.minimum(u, 0.0) - d)
            d = (k[b] + kn) * pn[b]
            u = 2.0 * n_v[z, :, col(b)] * pn[b]
            an.append(jnp.maximum(u, 0.0) + d)
            bn.append(jnp.minimum(u, 0.0) - d)
        aw, bw = west_of(ae, True), west_of(be, True)
        coef = [[], [], [], [], []]
        for b in range(NB):
            a_s, b_s = pltpu.roll(an[b], 1, 0), pltpu.roll(bn[b], 1, 0)
            c0 = keep[b] - (ae[b] - bw[b]) - (an[b] - b_s)
            for n, val in enumerate((c0, -be[b], aw[b], -bn[b], a_s)):
                coef[n].append(val)
                coefs[n, b, z] = val

        def put(b, r, j, val):
            first[b, r, z] = val

        stencil(
            lambda b, r, zz: q_v[r, zz, :, col(b)], coef, z, [mix[b] for b in range(NB)], put,
        )

    zero = jnp.zeros((NY, L), F32)

    def chunk(i, carry):
        @pl.when(i < NC - 1)
        def _():
            for cp in fetch(jnp.minimum(i + 1, NC - 1)):
                cp.wait()

        def body(h, _):
            level(i * CH + h)
            return 0

        lax.fori_loop(0, CH, body, 0, unroll=UNROLL1)
        for cp in store(i):
            cp.start()
        he, hw = carry
        for r in range(NR):
            acc_e, acc_w = zero, zero
            for h in range(CH):
                acc_e = to_lane(acc_e, first[NB - 1, r, i * CH + h], h, L - 1)
                acc_w = to_lane(acc_w, first[0, r, i * CH + h], h, 0)
            he = he + pltpu.roll(acc_e, r * NZ + i * CH, 1)
            hw = hw + pltpu.roll(acc_w, r * NZ + i * CH, 1)
        return he, hw

    cols[0], cols[1] = lax.fori_loop(0, NC, chunk, (zero, zero))
    ff = first.reshape(NB * NQ * NY, L)
    for b in range(NB):
        for g in range(0, NQ, 8):
            at = (b * NQ + g) * NY
            rows[0, b, g : g + 8, :] = ff[pl.ds(at + NY - 1, 8, stride=NY), :]
            rows[1, b, g : g + 8, :] = ff[pl.ds(at, 8, stride=NY), :]
    for i in range(NC):
        for cp in store(i):
            cp.wait()


def spread3(x):
    x = jnp.where(lanes() < NZ, x, 0.0)
    return x + pltpu.roll(x, NZ, 1) + pltpu.roll(x, 2 * NZ, 1)


def face(w_a, w_b, k_a, k_b, u):
    p = w_a * w_b
    d = 0.5 * (k_a + k_b) * p
    s = u * p
    return spread3(jnp.maximum(s, 0.0) + d), spread3(jnp.minimum(s, 0.0) - d)


def remap_kernel(
    idx, src, live, coup, got, tiles_h, wet, hown, rows_in, cols, edge_n, edge_s, r1, r2,
    forcing, ns1, ns2, ew1, ew2, hnew, facec, fluxes1, rows, facey, fluxy,
    tiles, sem,
):
    def fetch(i):
        at = pl.ds(i * NB, NB)
        return pltpu.make_async_copy(tiles_h.at[at], tiles.at[at], sem.at[i])

    for i in range(NY):
        fetch(i).start()
    row = subl()
    zero = jnp.zeros((NY, L), F32)
    cvec = []
    for r in range(NR):
        c = zero
        for f in range(10):
            c = jnp.where(row == f, coup[r, f], c)
        cvec.append(c)

    def target_row(i, _):
        fetch(i).wait()
        for s in range(NB):
            t = i * NB + s
            n = live[t]
            parts = []
            for k in range(4):
                p = src[k, t]
                blk = got[p // 6 * 8 + p % 6]
                parts.append(jnp.where(k < n, blk, jnp.zeros_like(blk)))
            acc = jnp.dot(jnp.concatenate(parts, axis=1), tiles[t], preferred_element_type=F32)
            for r in range(NR):
                forcing[s, r, pl.ds(i, 1), :] = jnp.sum(acc * cvec[r], axis=0, keepdims=True)
        return 0

    lax.fori_loop(0, NY, target_row, 0, unroll=4)
    for s in range(NB):
        w = wet[:, col(s)].astype(F32)
        for r in range(NR):
            forcing[s, r] = forcing[s, r] * w
    l_east, l_west = idx[2], idx[3]
    oe0, oe1, ow0, ow1 = hown[0], hown[1], hown[2], hown[3]
    ge0, ge1 = got[l_east * 8 + 6].astype(F32), got[l_east * 8 + 7].astype(F32)
    gw0, gw1 = got[l_west * 8 + 6].astype(F32), got[l_west * 8 + 7].astype(F32)

    def wcol(x):
        return jnp.broadcast_to(x[:, NQ : NQ + 1], (NY, L))

    ae, be = face(wcol(oe0), wcol(ge0), oe1, ge1, pltpu.roll(oe1, L - NZ, 1))
    aw, bw = face(wcol(gw0), wcol(ow0), gw1, ow1, pltpu.roll(gw1, L - NZ, 1))
    facec[0], facec[1], facec[2], facec[3] = ae, be, aw, bw
    fe = ae * oe0 + be * ge0
    fw = aw * gw0 + bw * ow0
    fluxes1[0], fluxes1[1] = fe, fw
    lane = lanes()
    for b in range(NB):
        hn_w, hs_w = from_sides(idx, r1, r2, (b, slice(192, 208)))
        pn = edge_n[b, 200:208, :] * hn_w[8:16]
        ps = hs_w[8:16] * edge_s[b, 200:208, :]
        fluxy[0, b, 120:128, :] = jnp.zeros((8, L), F32)
        fluxy[1, b, 120:128, :] = jnp.zeros((8, L), F32)
        halves = {}

        def halo(at):
            g = at // 16 * 16
            if g not in halves:
                halves[g] = from_sides(idx, r1, r2, (b, slice(g, g + 16)))
            n, s = halves[g]
            return n[at - g : at - g + 8], s[at - g : at - g + 8]

        for g in range(0, NZ, 8):
            kk, nn = slice(NQ + g, NQ + g + 8), slice(NQ + NZ + g, NQ + NZ + g + 8)
            kn, ks = halo(NQ + g)
            _, sn = halo(NQ + NZ + g)
            d, u = 0.5 * (edge_n[b, kk, :] + kn) * pn, edge_n[b, nn, :] * pn
            a_n, b_n = jnp.maximum(u, 0.0) + d, jnp.minimum(u, 0.0) - d
            d, u = 0.5 * (ks + edge_s[b, kk, :]) * ps, sn * ps
            a_s, b_s = jnp.maximum(u, 0.0) + d, jnp.minimum(u, 0.0) - d
            for n, val in enumerate((a_n, b_n, a_s, b_s)):
                facey[n, b, g : g + 8, :] = val
            for r in range(NR):
                j = r * NZ + g
                qn, qs = halo(j)
                fluxy[0, b, j : j + 8, :] = a_n * edge_n[b, j : j + 8, :] + b_n * qn
                fluxy[1, b, j : j + 8, :] = a_s * qs + b_s * edge_s[b, j : j + 8, :]
    he, hw = cols[0] - fe, cols[1] + fw
    for side, y, sign in ((0, NY - 1, -1.0), (1, 0, 1.0)):
        he = he + jnp.where(row == y, sign * fluxy[side, NB - 1].T[L - 1 : L, :], 0.0)
        hw = hw + jnp.where(row == y, sign * fluxy[side, 0].T[0:1, :], 0.0)
    for r in range(NR):
        here = lane == r * NZ
        he = he + jnp.where(here, pltpu.roll(forcing[4, r], r * NZ + 1, 1), 0.0)
        hw = hw + jnp.where(here, pltpu.roll(forcing[0, r], r * NZ, 1), 0.0)
    hnew[0], hnew[1] = he, hw
    leven = idx[1] == 1
    ew1[...] = jnp.where(leven, he, hw).astype(BF)
    ew2[...] = jnp.where(leven, hw, he).astype(BF)
    fill = jnp.zeros((L - NY, L), F32)
    fet = jnp.concatenate([fe, fill], axis=0).T
    fwt = jnp.concatenate([fw, fill], axis=0).T
    even = idx[0] == 1
    big = lanes(L)
    sub = subl(L)
    for b in range(NB):
        edges = []
        for side, y in ((0, NY - 1), (1, 0)):
            v = rows_in[side, b] + (fluxy[1, b] if side else -fluxy[0, b])
            for r in range(NR):
                v = v + jnp.where(sub == r * NZ, jnp.broadcast_to(forcing[b, r, y : y + 1, :], (L, L)), 0.0)
            if b == NB - 1:
                v = v - jnp.where(big == L - 1, jnp.broadcast_to(fet[:, y : y + 1], (L, L)), 0.0)
            if b == 0:
                v = v + jnp.where(big == 0, jnp.broadcast_to(fwt[:, y : y + 1], (L, L)), 0.0)
            rows[side, b] = v
            edges.append(v)
        n, s = edges
        ns1[b] = jnp.where(even, n, s).astype(BF)
        ns2[b] = jnp.where(even, s, n).astype(BF)


def step2_kernel(
    idx, r1, r2, g1, g2, wet, forcing, hnew, facec, fluxes1, rows, facey, fluxy, coefs, first_h,
    out_h,
    over_n, over_s, first, out_v, dl, mix, sem, osem,
):
    def copy(i, b):
        zs = pl.ds(i * CH, CH)
        return pltpu.make_async_copy(out_v.at[b, :, zs], out_h.at[:, zs, :, pl.ds(b * L, L)], osem.at[i, b])

    def fetch(i):
        zs = pl.ds(i * CH, CH)
        return pltpu.make_async_copy(first_h.at[:, :, zs], first.at[:, :, zs], sem.at[i])

    for i in range(NC):
        fetch(i).start()
    for b in range(NB):
        for g in range(0, NQ, 8):
            if g % 16 == 0:
                pair = from_sides(idx, r1, r2, (b, slice(g, g + 16)))
            hn, hs = pair[0][g % 16 : g % 16 + 8], pair[1][g % 16 : g % 16 + 8]
            a_n, b_n, a_s, b_s = (facey[n, b, g % NZ : g % NZ + 8, :] for n in range(4))
            over_n[b, g : g + 8, :] = a_n * rows[0, b, g : g + 8, :] + b_n * hn
            over_s[b, g : g + 8, :] = a_s * hs + b_s * rows[1, b, g : g + 8, :]
    leven = idx[1] == 1
    a, c = g1[...].astype(F32), g2[...].astype(F32)
    from_e, from_w = jnp.where(leven, a, c), jnp.where(leven, c, a)
    dl[0] = facec[0] * hnew[0] + facec[1] * from_e
    dl[1] = facec[2] * from_w + facec[3] * hnew[1]
    for b in range(NB):
        mix[b] = VMIX * wet[:, col(b)].astype(F32)
    lane = lanes()

    def ready(i):
        fetch(i).wait()
        for r in range(NR):
            back = L - (r * NZ + i * CH)
            over_e, over_w = pltpu.roll(fluxes1[0], back, 1), pltpu.roll(fluxes1[1], back, 1)
            for h in range(CH):
                z = i * CH + h
                at = pl.ds(r * NZ + z, 1)
                for b in range(NB):
                    v = add_rows(first[b, r, z], fluxy[1, b, at, :], fluxy[0, b, at, :])
                    if b == 0:
                        v = v + jnp.where(lane == 0, pltpu.roll(over_w, (L - h) % L, 1), 0.0)
                    if b == NB - 1:
                        v = v - jnp.where(lane == L - 1, pltpu.roll(over_e, L - 1 - h, 1), 0.0)
                    first[b, r, z] = v

    ready(0)
    for b in range(NB):
        for r in range(NR):
            first[b, r, 0] = first[b, r, 0] + forcing[b, r]

    def level(h, z, over_e, over_w):
        coef = [[coefs[n, b, z] for b in range(NB)] for n in range(5)]

        def put(b, r, j, val):
            if b == 0:
                val = val + jnp.where(lane == 0, pltpu.roll(over_w[r], (L - h) % L, 1), 0.0)
            if b == NB - 1:
                val = val - jnp.where(lane == L - 1, pltpu.roll(over_e[r], L - 1 - h, 1), 0.0)
            at = pl.ds(j, 1)
            out_v[b, r, z] = add_rows(val, over_s[b, at, :], over_n[b, at, :])

        stencil(lambda b, r, zz: first[b, r, zz], coef, z, [mix[b] for b in range(NB)], put)

    def chunk(i, _):
        @pl.when(i < NC - 1)
        def _():
            ready(jnp.minimum(i + 1, NC - 1))

        over_e = [pltpu.roll(dl[0], L - (r * NZ + i * CH), 1) for r in range(NR)]
        over_w = [pltpu.roll(dl[1], L - (r * NZ + i * CH), 1) for r in range(NR)]
        for h in range(CH):
            level(h, i * CH + h, over_e, over_w)

        @pl.when(i == 0)
        def _():
            for b in range(NB):
                for r in range(NR):
                    out_v[b, r, 0] = out_v[b, r, 0] + forcing[b, r]

        for b in range(NB):
            copy(i, b).start()
        return 0

    lax.fori_loop(0, NC, chunk, 0)
    for i in range(NC):
        for b in range(NB):
            copy(i, b).wait()


def vmem(x):
    return pltpu.with_memory_space_constraint(x, pltpu.VMEM)


def hbm(x):
    return pltpu.with_memory_space_constraint(x, pltpu.HBM)


def shards(
    fluxes, tracers, diffusivity, east_speed, north_speed, wet, coupling, sources, live_slots, tiles
):
    sds = jax.ShapeDtypeStruct
    band, lon = lax.axis_index("comp"), lax.axis_index("lon")
    n_lon = lax.axis_size("lon")
    idx = jnp.stack([1 - band % 2, 1 - lon % 2, (lon + 1) % n_lon, (lon + n_lon - 1) % n_lon]).astype(jnp.int32)
    dma = pltpu.SemaphoreType.DMA
    q5, s5 = (NB, NR, NZ, NY, L), (NB, NZ, NY, L)
    cf = (5, NB, NZ, NY, L)
    nat, nats, tile = (NR, NZ, NY, 640), (NZ, NY, 640), (NB, NY, L)
    rowpay, edgepay = (NB, 208, L), (NB, 128, L)

    def params(mib):
        return pltpu.CompilerParams(vmem_limit_bytes=mib << 20)

    def cost(us):
        return pl.CostEstimate(flops=0, transcendentals=0, bytes_accessed=us * 3_000_000)

    flux, q, k, e, n, wh = map(
        hbm, (fluxes[:, 0, :], tracers, diffusivity, east_speed, north_speed, wet)
    )
    a2a, ns1, ns2, hown, edge_n, edge_s = pl.pallas_call(
        pack_kernel,
        out_shape=(
            sds((16, 8, NY, L), BF), sds(rowpay, BF), sds(rowpay, BF), sds((4, NY, L), F32),
            sds(rowpay, F32), sds(rowpay, F32),
        ),
        in_specs=[SM] + [ANY] * 6,
        out_specs=(VM,) * 6,
        scratch_shapes=[
            pltpu.VMEM((10, 12288), BF), pltpu.VMEM(q5, F32), pltpu.VMEM(s5, F32), pltpu.VMEM(s5, F32),
            pltpu.VMEM((NZ, NY, L), F32), pltpu.VMEM((NY, 640), jnp.int32), dma((18,)),
        ],
        cost_estimate=cost(6),
        compiler_params=params(20),
        name="pack",
    )(idx, flux, q, k, e, n, wh)
    swap_a = [(i, i ^ 1) for i in range(8)]
    swap_b = [(i, i + 1) for i in (1, 3, 5)] + [(i + 1, i) for i in (1, 3, 5)]
    r1 = lax.ppermute(ns1, "comp", swap_a)
    r2 = lax.ppermute(ns2, "comp", swap_b)
    got = lax.all_to_all(a2a, "lon", split_axis=0, concat_axis=0, tiled=True)
    first, coefs, rows, cols = pl.pallas_call(
        step1_kernel,
        out_shape=(pltpu.HBM(q5, F32), pltpu.HBM(cf, F32), sds((2,) + edgepay, F32), sds((2, NY, L), F32)),
        in_specs=[ANY] * 5,
        out_specs=(ANY,) * 2 + (VM,) * 2,
        scratch_shapes=[
            pltpu.VMEM(nat, F32), pltpu.VMEM(nats, F32), pltpu.VMEM(nats, F32), pltpu.VMEM(nats, F32),
            pltpu.VMEM(q5, F32), pltpu.VMEM(cf, F32),
            pltpu.VMEM((NY, 640), jnp.int32),
            pltpu.VMEM(tile, F32), pltpu.VMEM(tile, F32), pltpu.VMEM(tile, F32), pltpu.VMEM(tile, F32),
            dma((NC + 1, 4)), dma((NC, 2)),
        ],
        cost_estimate=cost(30),
        compiler_params=params(28),
        name="step1",
    )(wh, q, k, e, n)
    forcing, ms1, ms2, ew1, ew2, hnew, facec, fluxes1, rows, facey, fluxy = pl.pallas_call(
        remap_kernel,
        out_shape=(
            sds((NB, NR, NY, L), F32), sds(edgepay, BF), sds(edgepay, BF), sds((NY, L), BF), sds((NY, L), BF),
            sds((2, NY, L), F32), sds((4, NY, L), F32), sds((2, NY, L), F32),
            sds((2,) + edgepay, F32), sds((4, NB, NZ, L), F32), sds((2,) + edgepay, F32),
        ),
        in_specs=[SM] * 4 + [VM, ANY] + [VM] * 8,
        out_specs=(VM,) * 11,
        scratch_shapes=[pltpu.VMEM((80, 512, L), BF), dma((NY,))],
        cost_estimate=cost(7),
        compiler_params=params(20),
        name="remap",
    )(idx, sources.T, live_slots, coupling, got.reshape(128, NY, L), hbm(tiles.reshape(80, 512, L)), wet, hown, rows, cols,
      edge_n, edge_s, r1, r2)
    lon_a = [(i, i ^ 1) for i in range(16)]
    lon_b = [((2 * i + 1) % 16, (2 * i + 2) % 16) for i in range(8)]
    lon_b = lon_b + [(b, a) for a, b in lon_b]
    r1 = lax.ppermute(ms1, "comp", swap_a)
    r2 = lax.ppermute(ms2, "comp", swap_b)
    g1 = lax.ppermute(ew1, "lon", lon_a)
    g2 = lax.ppermute(ew2, "lon", lon_b)
    return pl.pallas_call(
        step2_kernel,
        out_shape=sds(tracers.shape, F32),
        in_specs=[SM] + [VM] * 13 + [ANY],
        out_specs=ANY,
        scratch_shapes=[
            pltpu.VMEM(edgepay, F32), pltpu.VMEM(edgepay, F32), pltpu.VMEM(q5, F32), pltpu.VMEM(q5, F32),
            pltpu.VMEM((2, NY, L), F32), pltpu.VMEM(tile, F32), dma((NC,)), dma((NC, NB)),
        ],
        cost_estimate=cost(7),
        compiler_params=params(14),
        name="step2",
    )(idx, r1, r2, g1, g2, wet, forcing, hnew, facec, fluxes1, rows, facey, fluxy, vmem(coefs), hbm(first))


def solution(mesh):
    return jax.shard_map(
        shards,
        mesh=mesh,
        in_specs=(
            P(None, ("comp", "lon"), None),
            P(None, None, "comp", "lon"),
            P(None, "comp", "lon"),
            P(None, "comp", "lon"),
            P(None, "comp", "lon"),
            P("comp", "lon"),
            P(),
            P(("comp", "lon"), None),
            P(("comp", "lon")),
            P(("comp", "lon"), None, None, None),
        ),
        out_specs=P(None, None, "comp", "lon"),
        check_vma=False,
    )
```

time: 87.1 us -> 60 us (0.69)
  local copies, waits for them, and re-layouts: 12 us -> 0.02 us
  waiting for transfers between devices: 11.2 us -> 1.34 us
  Pallas kernels: 39.8 us -> 34.8 us
    unnamed x18 -> x10, local copies, waits for them, and re-layouts: 12 us -> 0.02 us
    pallas_call x4 -> x3, Pallas kernels: 35.1 us -> 27.4 us  [the longest x1 12.7 us: shards(): pl.pallas_call(step1_kernel, out_shape=(pltpu.HBM(q5, F32), pltpu.HBM(cf,...]
    ppermute x1, waiting for transfers between devices: 7.12 us -> 0.01 us  [shards(): r2 = lax.ppermute(ns2, 'comp', swap_b)]
    ppermute x1, starting transfers between devices: 7.67 us -> 4.31 us  [shards(): r2 = lax.ppermute(ms2, 'comp', swap_b)]
    pallas_call x1, Pallas kernels: 4.71 us -> 7.38 us  [shards(): pl.pallas_call(remap_kernel, out_shape=(sds((NB, NR, NY, L), F32), sds(ed...]
    ppermute x1, starting transfers between devices: 4 us -> 6.17 us  [shards(): g2 = lax.ppermute(ew2, 'lon', lon_b)]
    ppermute x1, waiting for transfers between devices: 2.72 us -> 1.33 us  [shards(): g2 = lax.ppermute(ew2, 'lon', lon_b)]
    ppermute x1, waiting for transfers between devices: 1.31 us -> 0.01 us  [shards(): r1 = lax.ppermute(ns1, 'comp', swap_a)]
  transfers between devices with their start and end apart: 7 -> 7, of which waited for: 3 -> 1; matrix products, arithmetic and copies ran while one was open for 0% -> 0% of each run, Pallas kernels for 18% -> 21%
where the time goes in v1:
time: 60 us; the launch traced here: 59.7 us
  Pallas kernels  34.8 us (58%)
  starting transfers between devices  23.4 us (39%)
  waiting for transfers between devices  1.34 us (2%)
    pallas_call x1, Pallas kernels, shards(): pl.pallas_call(step1_kernel, out_shape=(pltpu.HBM(q5, F32), pltpu.HBM(cf,...  12.7 us
    pallas_call x1, Pallas kernels, shards(): pl.pallas_call(step2_kernel, out_shape=sds(tracers.shape, F32), in_specs=...  9.36 us
    all_to_all x1, starting transfers between devices, shards(): got = lax.all_to_all(a2a, 'lon', split_axis=0, concat_axis=0, tiled=True)  7.9 us
    pallas_call x1, Pallas kernels, shards(): pl.pallas_call(remap_kernel, out_shape=(sds((NB, NR, NY, L), F32), sds(ed...  7.38 us
    ppermute x1, starting transfers between devices, shards(): g2 = lax.ppermute(ew2, 'lon', lon_b)  6.17 us
    pallas_call x1, Pallas kernels, shards(): pl.pallas_call(pack_kernel, out_shape=(sds((16, 8, NY, L), BF), sds(rowpa...  5.33 us
    ppermute x1, starting transfers between devices, shards(): r2 = lax.ppermute(ms2, 'comp', swap_b)  4.31 us
    ppermute x1, starting transfers between devices, shards(): r2 = lax.ppermute(ns2, 'comp', swap_b)  4.19 us
  transfers between devices with their start and end apart: 7, of which 1 were waited for; matrix products, arithmetic and copies ran while one was open for 0% of the time, Pallas kernels for 21%

profile of v1, /device:TPU:2, one launch (start us, length us, event | category | flops | bytes accessed | tf_op | source)
XLA Modules:
  0.0 59.7 jit_solution(17487511766775575568)
XLA Ops:
  0.0 0.1 pad_add_fusion.idx
  0.1 5.3 %pack.1 = (bf16[16,8,16,128]{3,2,1,0:T(8,128)(2,1)}, bf16[5,208,128]{2,1,0:T(8,128)(2,1)S(1)}, bf16[5,208,128]{2,1,0:T(8,128)(2,1)S(1)}, f32[4,16,128]{2,1,0:T(8...) custom-call(s32[4]{0:T(128)S(1)} %pad_add_fusion.idx, bf16[10,12288]{1,0:T(8,128)(2,1)} %bitcast.11, ...), custom_call_target="tpu_custom_call" | custom-call | bytes 18000000 | tf_op jit(solution)/shard_map/pack/pallas_call | solution.py:522
  5.4 7.9 %all-to-all-start = ((bf16[16,8,16,128]{3,2,1,0:T(8,128)(2,1)}), bf16[16,8,16,128]{3,2,1,0:T(8,128)(2,1)S(1)}, u32[]{:S(2)}, u32[]{:S(2)}) async-start(bf16[16,8,16,128]{3,2,1,0:T(8,128)(2,1)} %get-tuple-element.26), calls=%async_computation | async-start | bytes 1048576 | tf_op jit(solution)/shard_map/all_to_all | solution.py:542
  13.3 0.6 %collective-permute-start = (bf16[5,208,128]{2,1,0:T(8,128)(2,1)S(1)}, bf16[5,208,128]{2,1,0:T(8,128)(2,1)S(1)}, u32[]{:S(2)}, u32[]{:S(2)}) collective-permute-start(bf16[5,208,128]{2,1,0:T(8,128)(2,1)S(1)} %get-tuple-element.32), channel_id=1, source_target_pairs={{0,16},{16,0},{32,48},{48,32},{64,80},{80,64},{96,112},{112,96},{1... | collective-permute-start | bytes 798728 | tf_op jit(solution)/shard_map/ppermute | solution.py:540
  13.9 4.2 %collective-permute-start.1 = (bf16[5,208,128]{2,1,0:T(8,128)(2,1)S(1)}, bf16[5,208,128]{2,1,0:T(8,128)(2,1)S(1)}, u32[]{:S(2)}, u32[]{:S(2)}) collective-permute-start(bf16[5,208,128]{2,1,0:T(8,128)(2,1)S(1)} %get-tuple-element.33), channel_id=1, source_target_pairs={{16,32},{48,64},{80,96},{32,16},{64,48},{96,80},{17,33},{49,65},{8... | collective-permute-start | bytes 798728 | tf_op jit(solution)/shard_map/ppermute | solution.py:541
  18.1 12.7 %step1.1 = (f32[5,3,40,16,128]{4,3,2,1,0:T(8,128)}, f32[5,5,40,16,128]{4,3,2,1,0:T(8,128)}, f32[2,5,128,128]{3,2,1,0:T(8,128)S(1)}, f32[2,16,128]{2,1,0:T(8,128)S(1)}) custom-call(s32[16,640]{1,0:T(8,128)} %wet.3, f32[3,40,16,640]{3,2,1,0:T(8,128)} %q_h.3, f32[40,16,640]{2,1,0:T(8,128)} %k_h.3, f32[40,16,640]{2,1,0:T(8,128)} %e_h.3, f32[40,16,640]{2,1,0:T(8,128)} %n_h.3), custom_call_target="tpu_custom_call" | custom-call | bytes 90000000 | tf_op jit(solution)/shard_map/step1/pallas_call | solution.py:543
  30.9 0.0 collective-permute-done.r1
  30.9 0.0 collective-permute-done.1.r2
  30.9 0.0 all-to-all-done
  30.9 0.0 copy-done.1
  30.9 0.0 copy-done.2
  30.9 0.0 copy-done.3
  30.9 0.0 copy-done.4
  30.9 0.0 copy-start
  31.0 7.4 %remap.1 = (f32[5,3,16,128]{3,2,1,0:T(8,128)S(1)}, bf16[5,128,128]{2,1,0:T(8,128)(2,1)S(1)}, bf16[5,128,128]{2,1,0:T(8,128)(2,1)S(1)}, bf16[16,128]{1,0:T(8,128)...) custom-call(s32[4]{0:T(128)S(1)} %pad_add_fusion.idx, ...), custom_call_target="tpu_custom_call" | custom-call | bytes 21000000 | tf_op jit(solution)/shard_map/remap/pallas_call | solution.py:559
  38.3 0.1 collective-permute-start.2
  38.4 4.3 %collective-permute-start.3 = (bf16[5,128,128]{2,1,0:T(8,128)(2,1)S(1)}, bf16[5,128,128]{2,1,0:T(8,128)(2,1)S(1)}, u32[]{:S(2)}, u32[]{:S(2)}) collective-permute-start(bf16[5,128,128]{2,1,0:T(8,128)(2,1)S(1)} %get-tuple-element.35), channel_id=1, source_target_pairs={{16,32},{48,64},{80,96},{32,16},{64,48},{96,80},{17,33},{49,65},{8... | collective-permute-start | bytes 491528 | tf_op jit(solution)/shard_map/ppermute | solution.py:578
  42.8 0.1 collective-permute-start.4
  42.8 6.2 %collective-permute-start.5 = (bf16[16,128]{1,0:T(8,128)(2,1)S(1)}, bf16[16,128]{1,0:T(8,128)(2,1)S(1)}, u32[]{:S(2)}, u32[]{:S(2)}) collective-permute-start(bf16[16,128]{1,0:T(8,128)(2,1)S(1)} %get-tuple-element.37), channel_id=1, source_target_pairs={{1,2},{3,4},{5,6},{7,8},{9,10},{11,12},{13,14},{15,0},{2,1},{4,3},... | collective-permute-start | bytes 12296 | tf_op jit(solution)/shard_map/ppermute | solution.py:580
  49.0 0.0 collective-permute-done.4.g1
  49.0 1.3 %collective-permute-done.5.g2 = bf16[16,128]{1,0:T(8,128)(2,1)S(1)} collective-permute-done((bf16[16,128]{1,0:T(8,128)(2,1)S(1)}, bf16[16,128]{1,0:T(8,128)(2,1)S(1)}, u32[]{:S(2)}, u32[]{:S(2)}) %collective-permute-start.5) | collective-permute-done | bytes 4128 | tf_op jit(solution)/shard_map/ppermute | solution.py:580
  50.4 0.0 collective-permute-done.2.r1
  50.4 0.0 collective-permute-done.3.r2
  50.4 9.4 %step2.1 = f32[3,40,16,640]{3,2,1,0:T(8,128)} custom-call(s32[4]{0:T(128)S(1)} %pad_add_fusion.idx, bf16[5,128,128]{2,1,0:T(8,128)(2,1)S(1)} %collective-permute-done.2.r1, bf16[5,128,128]{2,1,0:T(8,128)(2,1)S(1)} %collective-permute-done.3.r2, bf16[16,128]{1,0:T(8,128)(2,1)S(1)} %collective-permute-done.4.g1, ...), custom_call_target="tpu_custom_call" | custom-call | bytes 21000000 | tf_op jit(solution)/shard_map/step2/pallas_call | solution.py:581
  (5 shorter events, 0.0 us)
Async XLA Ops:
  5.4 25.5 %all-to-all-start = ((bf16[16,8,16,128]{3,2,1,0:T(8,128)(2,1)}), bf16[16,8,16,128]{3,2,1,0:T(8,128)(2,1)S(1)}, u32[]{:S(2)}, u32[]{:S(2)}) async-start(bf16[16,8,16,128]{3,2,1,0:T(8,128)(2,1)} %get-tuple-element.26), calls=%async_computation | async-start | bytes 1048576 | tf_op jit(solution)/shard_map/all_to_all | solution.py:542
  13.3 17.6 %collective-permute-start = (bf16[5,208,128]{2,1,0:T(8,128)(2,1)S(1)}, bf16[5,208,128]{2,1,0:T(8,128)(2,1)S(1)}, u32[]{:S(2)}, u32[]{:S(2)}) collective-permute-start(bf16[5,208,128]{2,1,0:T(8,128)(2,1)S(1)} %get-tuple-element.32), channel_id=1, source_target_pairs={{0,16},{16,0},{32,48},{48,32},{64,80},{80,64},{96,112},{112,96},{1... | collective-permute-start | bytes 798728 | tf_op jit(solution)/shard_map/ppermute | solution.py:540
  13.9 17.0 %copy-start.1 = (s32[16,640]{1,0:T(8,128)S(1)}, s32[16,640]{1,0:T(8,128)}, u32[]{:S(2)}) copy-start(s32[16,640]{1,0:T(8,128)} %wet.3) | copy-start | bytes 122884
  13.9 17.0 %copy-start.2 = (s32[80,4]{0,1:T(4,128)S(1)}, s32[80,4]{0,1:T(4,128)}, u32[]{:S(2)}) copy-start(s32[80,4]{0,1:T(4,128)} %param.17) | copy-start | bytes 3844
  13.9 17.0 %copy-start.3 = (f32[3,10]{1,0:T(4,128)S(1)}, f32[3,10]{1,0:T(4,128)}, u32[]{:S(2)}) copy-start(f32[3,10]{1,0:T(4,128)} %coup.1) | copy-start | bytes 364
  13.9 17.0 %copy-start.4 = (s32[80]{0:T(128)S(1)}, s32[80]{0:T(128)}, u32[]{:S(2)}) copy-start(s32[80]{0:T(128)} %live.1) | copy-start | bytes 964
  13.9 16.9 %collective-permute-start.1 = (bf16[5,208,128]{2,1,0:T(8,128)(2,1)S(1)}, bf16[5,208,128]{2,1,0:T(8,128)(2,1)S(1)}, u32[]{:S(2)}, u32[]{:S(2)}) collective-permute-start(bf16[5,208,128]{2,1,0:T(8,128)(2,1)S(1)} %get-tuple-element.33), channel_id=1, source_target_pairs={{16,32},{48,64},{80,96},{32,16},{64,48},{96,80},{17,33},{49,65},{8... | collective-permute-start | bytes 798728 | tf_op jit(solution)/shard_map/ppermute | solution.py:541
  30.9 19.4 %copy-start = (f32[5,5,40,16,128]{4,3,2,1,0:T(8,128)S(1)}, f32[5,5,40,16,128]{4,3,2,1,0:T(8,128)}, u32[]{:S(2)}) copy-start(f32[5,5,40,16,128]{4,3,2,1,0:T(8,128)} %get-tuple-element.45.coefs) | copy-start | bytes 24576004
  38.3 12.0 %collective-permute-start.2 = (bf16[5,128,128]{2,1,0:T(8,128)(2,1)S(1)}, bf16[5,128,128]{2,1,0:T(8,128)(2,1)S(1)}, u32[]{:S(2)}, u32[]{:S(2)}) collective-permute-start(bf16[5,128,128]{2,1,0:T(8,128)(2,1)S(1)} %get-tuple-element.34), channel_id=1, source_target_pairs={{0,16},{16,0},{32,48},{48,32},{64,80},{80,64},{96,112},{112,96},{1... | collective-permute-start | bytes 491528 | tf_op jit(solution)/shard_map/ppermute | solution.py:577
  38.4 11.9 %collective-permute-start.3 = (bf16[5,128,128]{2,1,0:T(8,128)(2,1)S(1)}, bf16[5,128,128]{2,1,0:T(8,128)(2,1)S(1)}, u32[]{:S(2)}, u32[]{:S(2)}) collective-permute-start(bf16[5,128,128]{2,1,0:T(8,128)(2,1)S(1)} %get-tuple-element.35), channel_id=1, source_target_pairs={{16,32},{48,64},{80,96},{32,16},{64,48},{96,80},{17,33},{49,65},{8... | collective-permute-start | bytes 491528 | tf_op jit(solution)/shard_map/ppermute | solution.py:578
  42.8 6.3 %collective-permute-start.4 = (bf16[16,128]{1,0:T(8,128)(2,1)S(1)}, bf16[16,128]{1,0:T(8,128)(2,1)S(1)}, u32[]{:S(2)}, u32[]{:S(2)}) collective-permute-start(bf16[16,128]{1,0:T(8,128)(2,1)S(1)} %get-tuple-element.36), channel_id=1, source_target_pairs={{0,1},{1,0},{2,3},{3,2},{4,5},{5,4},{6,7},{7,6},{8,9},{9,8},{10,11... | collective-permute-start | bytes 12296 | tf_op jit(solution)/shard_map/ppermute | solution.py:579
  42.8 7.5 %collective-permute-start.5 = (bf16[16,128]{1,0:T(8,128)(2,1)S(1)}, bf16[16,128]{1,0:T(8,128)(2,1)S(1)}, u32[]{:S(2)}, u32[]{:S(2)}) collective-permute-start(bf16[16,128]{1,0:T(8,128)(2,1)S(1)} %get-tuple-element.37), channel_id=1, source_target_pairs={{1,2},{3,4},{5,6},{7,8},{9,10},{11,12},{13,14},{15,0},{2,1},{4,3},... | collective-permute-start | bytes 12296 | tf_op jit(solution)/shard_map/ppermute | solution.py:580

commit v2 on v1

--- a/solution.py
+++ b/solution.py
@@ -18,7 +18,8 @@
 NQ = NR * NZ
 CH = 8
 NC = NZ // CH
-UNROLL1 = 2
+C1 = 4
+N1 = NZ // C1
 
 
 def lanes(rows=NY):
@@ -62,7 +63,7 @@
         copies[b] = [
             pltpu.make_async_copy(q_h.at[:, :, :, at], q_v.at[b], sem.at[3 + 3 * b]),
             pltpu.make_async_copy(k_h.at[:, :, at], k_v.at[b], sem.at[4 + 3 * b]),
-            pltpu.make_async_copy(n_h.at[:, :, at], n_v.at[b], sem.at[5 + 3 * b]),
+            pltpu.make_async_copy(n_h.at[:, pl.ds(8, 8), at], n_v.at[b], sem.at[5 + 3 * b]),
         ]
     for cp in first_two:
         cp.start()
@@ -117,12 +118,17 @@
         if b not in (4, 0):
             for cp in copies[b]:
                 cp.wait()
-        for ref, count, base in ((q_v, NQ, 0), (k_v, NZ, NQ), (n_v, NZ, NQ + NZ)):
+        for ref, count, base in ((q_v, NQ, 0), (k_v, NZ, NQ)):
             flat = ref.reshape(NB * count * NY, L)
             for g in range(0, count, 8):
                 at = (b * count + g) * NY
                 edge_n[b, base + g : base + g + 8, :] = flat[pl.ds(at + NY - 1, 8, stride=NY), :]
                 edge_s[b, base + g : base + g + 8, :] = flat[pl.ds(at, 8, stride=NY), :]
+        flat = n_v.reshape(NB * NZ * 8, L)
+        for g in range(0, NZ, 8):
+            top = flat[pl.ds((b * NZ + g) * 8 + 7, 8, stride=8), :]
+            edge_n[b, NQ + NZ + g : NQ + NZ + g + 8, :] = top
+            edge_s[b, NQ + NZ + g : NQ + NZ + g + 8, :] = top
         w = wet_i[:, col(b)].astype(F32)
         edge_n[b, 200:208, :] = jnp.broadcast_to(w[NY - 1 : NY, :], (8, L))
         edge_s[b, 200:208, :] = jnp.broadcast_to(w[0:1, :], (8, L))
@@ -163,11 +169,11 @@
     first_h, coefs_h, rows, cols,
     q_v, k_v, e_v, n_v, first, coefs, wet_i, pe, pn, keep, mix, sem, osem,
 ):
-    cw = pltpu.make_async_copy(wet_h, wet_i, sem.at[NC, 0])
+    cw = pltpu.make_async_copy(wet_h, wet_i, sem.at[N1, 0])
     cw.start()
 
     def fetch(i):
-        zs = pl.ds(i * CH, CH)
+        zs = pl.ds(i * C1, C1)
         return [
             pltpu.make_async_copy(q_h.at[:, zs], q_v.at[:, zs], sem.at[i, 0]),
             pltpu.make_async_copy(k_h.at[zs], k_v.at[zs], sem.at[i, 1]),
@@ -176,13 +182,13 @@
         ]
 
     def store(i):
-        zs = pl.ds(i * CH, CH)
+        zs = pl.ds(i * C1, C1)
         return [
             pltpu.make_async_copy(first.at[:, :, zs], first_h.at[:, :, zs], osem.at[i, 0]),
             pltpu.make_async_copy(coefs.at[:, :, zs], coefs_h.at[:, :, zs], osem.at[i, 1]),
         ]
 
-    for i in range(NC):
+    for i in range(N1):
         for cp in fetch(i):
             cp.start()
     cw.wait()
@@ -230,19 +236,24 @@
 
     zero = jnp.zeros((NY, L), F32)
 
-    def chunk(i, carry):
-        @pl.when(i < NC - 1)
+    def chunk(i, _):
+        @pl.when(i < N1 - 1)
         def _():
-            for cp in fetch(jnp.minimum(i + 1, NC - 1)):
+            for cp in fetch(jnp.minimum(i + 1, N1 - 1)):
                 cp.wait()
 
         def body(h, _):
-            level(i * CH + h)
+            level(i * C1 + h)
             return 0
 
-        lax.fori_loop(0, CH, body, 0, unroll=UNROLL1)
+        lax.fori_loop(0, C1, body, 0, unroll=4)
         for cp in store(i):
             cp.start()
+        return 0
+
+    lax.fori_loop(0, N1, chunk, 0)
+
+    def edge(i, carry):
         he, hw = carry
         for r in range(NR):
             acc_e, acc_w = zero, zero
@@ -253,14 +264,14 @@
             hw = hw + pltpu.roll(acc_w, r * NZ + i * CH, 1)
         return he, hw
 
-    cols[0], cols[1] = lax.fori_loop(0, NC, chunk, (zero, zero))
+    cols[0], cols[1] = lax.fori_loop(0, NC, edge, (zero, zero))
     ff = first.reshape(NB * NQ * NY, L)
     for b in range(NB):
         for g in range(0, NQ, 8):
             at = (b * NQ + g) * NY
             rows[0, b, g : g + 8, :] = ff[pl.ds(at + NY - 1, 8, stride=NY), :]
             rows[1, b, g : g + 8, :] = ff[pl.ds(at, 8, stride=NY), :]
-    for i in range(NC):
+    for i in range(N1):
         for cp in store(i):
             cp.wait()
 
@@ -290,33 +301,6 @@
         fetch(i).start()
     row = subl()
     zero = jnp.zeros((NY, L), F32)
-    cvec = []
-    for r in range(NR):
-        c = zero
-        for f in range(10):
-            c = jnp.where(row == f, coup[r, f], c)
-        cvec.append(c)
-
-    def target_row(i, _):
-        fetch(i).wait()
-        for s in range(NB):
-            t = i * NB + s
-            n = live[t]
-            parts = []
-            for k in range(4):
-                p = src[k, t]
-                blk = got[p // 6 * 8 + p % 6]
-                parts.append(jnp.where(k < n, blk, jnp.zeros_like(blk)))
-            acc = jnp.dot(jnp.concatenate(parts, axis=1), tiles[t], preferred_element_type=F32)
-            for r in range(NR):
-                forcing[s, r, pl.ds(i, 1), :] = jnp.sum(acc * cvec[r], axis=0, keepdims=True)
-        return 0
-
-    lax.fori_loop(0, NY, target_row, 0, unroll=4)
-    for s in range(NB):
-        w = wet[:, col(s)].astype(F32)
-        for r in range(NR):
-            forcing[s, r] = forcing[s, r] * w
     l_east, l_west = idx[2], idx[3]
     oe0, oe1, ow0, ow1 = hown[0], hown[1], hown[2], hown[3]
     ge0, ge1 = got[l_east * 8 + 6].astype(F32), got[l_east * 8 + 7].astype(F32)
@@ -362,6 +346,33 @@
                 qn, qs = halo(j)
                 fluxy[0, b, j : j + 8, :] = a_n * edge_n[b, j : j + 8, :] + b_n * qn
                 fluxy[1, b, j : j + 8, :] = a_s * qs + b_s * edge_s[b, j : j + 8, :]
+    cvec = []
+    for r in range(NR):
+        c = zero
+        for f in range(10):
+            c = jnp.where(row == f, coup[r, f], c)
+        cvec.append(c)
+
+    def target_row(i, _):
+        fetch(i).wait()
+        for s in range(NB):
+            t = i * NB + s
+            n = live[t]
+            parts = []
+            for k in range(4):
+                p = src[k, t]
+                blk = got[p // 6 * 8 + p % 6]
+                parts.append(jnp.where(k < n, blk, jnp.zeros_like(blk)))
+            acc = jnp.dot(jnp.concatenate(parts, axis=1), tiles[t], preferred_element_type=F32)
+            for r in range(NR):
+                forcing[s, r, pl.ds(i, 1), :] = jnp.sum(acc * cvec[r], axis=0, keepdims=True)
+        return 0
+
+    lax.fori_loop(0, NY, target_row, 0, unroll=4)
+    for s in range(NB):
+        w = wet[:, col(s)].astype(F32)
+        for r in range(NR):
+            forcing[s, r] = forcing[s, r] * w
     he, hw = cols[0] - fe, cols[1] + fw
     for side, y, sign in ((0, NY - 1, -1.0), (1, 0, 1.0)):
         he = he + jnp.where(row == y, sign * fluxy[side, NB - 1].T[L - 1 : L, :], 0.0)
@@ -398,20 +409,14 @@
 
 
 def step2_kernel(
-    idx, r1, r2, g1, g2, wet, forcing, hnew, facec, fluxes1, rows, facey, fluxy, coefs, first_h,
+    idx, r1, r2, g1, g2, wet, forcing, hnew, facec, fluxes1, rows, facey, fluxy, coefs, first_in,
     out_h,
-    over_n, over_s, first, out_v, dl, mix, sem, osem,
+    over_n, over_s, first, out_v, dl, mix, osem,
 ):
     def copy(i, b):
         zs = pl.ds(i * CH, CH)
         return pltpu.make_async_copy(out_v.at[b, :, zs], out_h.at[:, zs, :, pl.ds(b * L, L)], osem.at[i, b])
 
-    def fetch(i):
-        zs = pl.ds(i * CH, CH)
-        return pltpu.make_async_copy(first_h.at[:, :, zs], first.at[:, :, zs], sem.at[i])
-
-    for i in range(NC):
-        fetch(i).start()
     for b in range(NB):
         for g in range(0, NQ, 8):
             if g % 16 == 0:
@@ -430,7 +435,6 @@
     lane = lanes()
 
     def ready(i):
-        fetch(i).wait()
         for r in range(NR):
             back = L - (r * NZ + i * CH)
             over_e, over_w = pltpu.roll(fluxes1[0], back, 1), pltpu.roll(fluxes1[1], back, 1)
@@ -438,7 +442,7 @@
                 z = i * CH + h
                 at = pl.ds(r * NZ + z, 1)
                 for b in range(NB):
-                    v = add_rows(first[b, r, z], fluxy[1, b, at, :], fluxy[0, b, at, :])
+                    v = add_rows(first_in[b, r, z], fluxy[1, b, at, :], fluxy[0, b, at, :])
                     if b == 0:
                         v = v + jnp.where(lane == 0, pltpu.roll(over_w, (L - h) % L, 1), 0.0)
                     if b == NB - 1:
@@ -528,7 +532,7 @@
         in_specs=[SM] + [ANY] * 6,
         out_specs=(VM,) * 6,
         scratch_shapes=[
-            pltpu.VMEM((10, 12288), BF), pltpu.VMEM(q5, F32), pltpu.VMEM(s5, F32), pltpu.VMEM(s5, F32),
+            pltpu.VMEM((10, 12288), BF), pltpu.VMEM(q5, F32), pltpu.VMEM(s5, F32), pltpu.VMEM((NB, NZ, 8, L), F32),
             pltpu.VMEM((NZ, NY, L), F32), pltpu.VMEM((NY, 640), jnp.int32), dma((18,)),
         ],
         cost_estimate=cost(6),
@@ -550,7 +554,7 @@
             pltpu.VMEM(q5, F32), pltpu.VMEM(cf, F32),
             pltpu.VMEM((NY, 640), jnp.int32),
             pltpu.VMEM(tile, F32), pltpu.VMEM(tile, F32), pltpu.VMEM(tile, F32), pltpu.VMEM(tile, F32),
-            dma((NC + 1, 4)), dma((NC, 2)),
+            dma((N1 + 1, 4)), dma((N1, 2)),
         ],
         cost_estimate=cost(30),
         compiler_params=params(28),
@@ -581,16 +585,16 @@
     return pl.pallas_call(
         step2_kernel,
         out_shape=sds(tracers.shape, F32),
-        in_specs=[SM] + [VM] * 13 + [ANY],
+        in_specs=[SM] + [VM] * 14,
         out_specs=ANY,
         scratch_shapes=[
             pltpu.VMEM(edgepay, F32), pltpu.VMEM(edgepay, F32), pltpu.VMEM(q5, F32), pltpu.VMEM(q5, F32),
-            pltpu.VMEM((2, NY, L), F32), pltpu.VMEM(tile, F32), dma((NC,)), dma((NC, NB)),
+            pltpu.VMEM((2, NY, L), F32), pltpu.VMEM(tile, F32), dma((NC, NB)),
         ],
         cost_estimate=cost(7),
         compiler_params=params(14),
         name="step2",
-    )(idx, r1, r2, g1, g2, wet, forcing, hnew, facec, fluxes1, rows, facey, fluxy, vmem(coefs), hbm(first))
+    )(idx, r1, r2, g1, g2, wet, forcing, hnew, facec, fluxes1, rows, facey, fluxy, vmem(coefs), vmem(first))
 
 
 def solution(mesh):

time: 60 us -> 57.4 us (0.957)
  Pallas kernels: 34.8 us -> 32.2 us
    pallas_call x1, Pallas kernels: 12.7 us -> 11.1 us  [shards(): pl.pallas_call(step1_kernel, out_shape=(pltpu.HBM(q5, F32), pltpu.HBM(cf,...]
    pallas_call x1, Pallas kernels: 9.36 us -> 8.65 us  [shards(): pl.pallas_call(step2_kernel, out_shape=sds(tracers.shape, F32), in_specs=...]
  transfers between devices with their start and end apart: 7 -> 7, of which waited for: 1 -> 1; matrix products, arithmetic and copies ran while one was open for 0% -> 0% of each run, Pallas kernels for 21% -> 19%
where the time goes in v2:
time: 57.4 us; the launch traced here: 57.1 us
  Pallas kernels  32.2 us (56%)
  starting transfers between devices  23.4 us (41%)
  waiting for transfers between devices  1.34 us (2%)
    pallas_call x1, Pallas kernels, shards(): pl.pallas_call(step1_kernel, out_shape=(pltpu.HBM(q5, F32), pltpu.HBM(cf,...  11.1 us
    pallas_call x1, Pallas kernels, shards(): pl.pallas_call(step2_kernel, out_shape=sds(tracers.shape, F32), in_specs=...  8.65 us
    all_to_all x1, starting transfers between devices, shards(): got = lax.all_to_all(a2a, 'lon', split_axis=0, concat_axis=0, tiled=True)  7.9 us
    pallas_call x1, Pallas kernels, shards(): pl.pallas_call(remap_kernel, out_shape=(sds((NB, NR, NY, L), F32), sds(ed...  7.2 us
    ppermute x1, starting transfers between devices, shards(): g2 = lax.ppermute(ew2, 'lon', lon_b)  6.09 us
    pallas_call x1, Pallas kernels, shards(): pl.pallas_call(pack_kernel, out_shape=(sds((16, 8, NY, L), BF), sds(rowpa...  5.23 us
    ppermute x1, starting transfers between devices, shards(): r2 = lax.ppermute(ms2, 'comp', swap_b)  4.39 us
    ppermute x1, starting transfers between devices, shards(): r2 = lax.ppermute(ns2, 'comp', swap_b)  4.19 us
  transfers between devices with their start and end apart: 7, of which 1 were waited for; matrix products, arithmetic and copies ran while one was open for 0% of the time, Pallas kernels for 19%

profile of v2, /device:TPU:2, one launch (start us, length us, event | category | flops | bytes accessed | tf_op | source)
XLA Modules:
  0.0 57.1 jit_solution(6984572663198505278)
XLA Ops:
  0.0 0.1 pad_add_fusion.idx
  0.1 5.2 %pack.1 = (bf16[16,8,16,128]{3,2,1,0:T(8,128)(2,1)}, bf16[5,208,128]{2,1,0:T(8,128)(2,1)S(1)}, bf16[5,208,128]{2,1,0:T(8,128)(2,1)S(1)}, f32[4,16,128]{2,1,0:T(8...) custom-call(s32[4]{0:T(128)S(1)} %pad_add_fusion.idx, bf16[10,12288]{1,0:T(8,128)(2,1)} %bitcast.11, ...), custom_call_target="tpu_custom_call" | custom-call | bytes 18000000 | tf_op jit(solution)/shard_map/pack/pallas_call | solution.py:526
  5.3 7.9 %all-to-all-start = ((bf16[16,8,16,128]{3,2,1,0:T(8,128)(2,1)}), bf16[16,8,16,128]{3,2,1,0:T(8,128)(2,1)S(1)}, u32[]{:S(2)}, u32[]{:S(2)}) async-start(bf16[16,8,16,128]{3,2,1,0:T(8,128)(2,1)} %get-tuple-element.26), calls=%async_computation | async-start | bytes 1048576 | tf_op jit(solution)/shard_map/all_to_all | solution.py:546
  13.2 0.6 %collective-permute-start = (bf16[5,208,128]{2,1,0:T(8,128)(2,1)S(1)}, bf16[5,208,128]{2,1,0:T(8,128)(2,1)S(1)}, u32[]{:S(2)}, u32[]{:S(2)}) collective-permute-start(bf16[5,208,128]{2,1,0:T(8,128)(2,1)S(1)} %get-tuple-element.32), channel_id=1, source_target_pairs={{0,16},{16,0},{32,48},{48,32},{64,80},{80,64},{96,112},{112,96},{1... | collective-permute-start | bytes 798728 | tf_op jit(solution)/shard_map/ppermute | solution.py:544
  13.8 4.2 %collective-permute-start.1 = (bf16[5,208,128]{2,1,0:T(8,128)(2,1)S(1)}, bf16[5,208,128]{2,1,0:T(8,128)(2,1)S(1)}, u32[]{:S(2)}, u32[]{:S(2)}) collective-permute-start(bf16[5,208,128]{2,1,0:T(8,128)(2,1)S(1)} %get-tuple-element.33), channel_id=1, source_target_pairs={{16,32},{48,64},{80,96},{32,16},{64,48},{96,80},{17,33},{49,65},{8... | collective-permute-start | bytes 798728 | tf_op jit(solution)/shard_map/ppermute | solution.py:545
  18.1 11.1 %step1.1 = (f32[5,3,40,16,128]{4,3,2,1,0:T(8,128)}, f32[5,5,40,16,128]{4,3,2,1,0:T(8,128)}, f32[2,5,128,128]{3,2,1,0:T(8,128)S(1)}, f32[2,16,128]{2,1,0:T(8,128)S(1)}) custom-call(s32[16,640]{1,0:T(8,128)} %wet.3, f32[3,40,16,640]{3,2,1,0:T(8,128)} %q_h.3, f32[40,16,640]{2,1,0:T(8,128)} %k_h.3, f32[40,16,640]{2,1,0:T(8,128)} %e_h.3, f32[40,16,640]{2,1,0:T(8,128)} %n_h.3), custom_call_target="tpu_custom_call" | custom-call | bytes 90000000 | tf_op jit(solution)/shard_map/step1/pallas_call | solution.py:547
  29.1 0.0 collective-permute-done.r1
  29.1 0.0 collective-permute-done.1.r2
  29.2 0.0 all-to-all-done
  29.2 0.0 copy-done.2
  29.2 0.0 copy-done.3
  29.2 0.0 copy-done.4
  29.2 0.0 copy-done.5
  29.2 0.0 copy-start.1
  29.2 7.2 %remap.1 = (f32[5,3,16,128]{3,2,1,0:T(8,128)S(1)}, bf16[5,128,128]{2,1,0:T(8,128)(2,1)S(1)}, bf16[5,128,128]{2,1,0:T(8,128)(2,1)S(1)}, bf16[16,128]{1,0:T(8,128)...) custom-call(s32[4]{0:T(128)S(1)} %pad_add_fusion.idx, ...), custom_call_target="tpu_custom_call" | custom-call | bytes 21000000 | tf_op jit(solution)/shard_map/remap/pallas_call | solution.py:563
  36.4 0.1 collective-permute-start.2
  36.5 4.4 %collective-permute-start.3 = (bf16[5,128,128]{2,1,0:T(8,128)(2,1)S(1)}, bf16[5,128,128]{2,1,0:T(8,128)(2,1)S(1)}, u32[]{:S(2)}, u32[]{:S(2)}) collective-permute-start(bf16[5,128,128]{2,1,0:T(8,128)(2,1)S(1)} %get-tuple-element.35), channel_id=1, source_target_pairs={{16,32},{48,64},{80,96},{32,16},{64,48},{96,80},{17,33},{49,65},{8... | collective-permute-start | bytes 491528 | tf_op jit(solution)/shard_map/ppermute | solution.py:582
  40.9 0.1 collective-permute-start.4
  41.0 6.1 %collective-permute-start.5 = (bf16[16,128]{1,0:T(8,128)(2,1)S(1)}, bf16[16,128]{1,0:T(8,128)(2,1)S(1)}, u32[]{:S(2)}, u32[]{:S(2)}) collective-permute-start(bf16[16,128]{1,0:T(8,128)(2,1)S(1)} %get-tuple-element.37), channel_id=1, source_target_pairs={{1,2},{3,4},{5,6},{7,8},{9,10},{11,12},{13,14},{15,0},{2,1},{4,3},... | collective-permute-start | bytes 12296 | tf_op jit(solution)/shard_map/ppermute | solution.py:584
  47.1 0.0 collective-permute-done.4.g1
  47.1 1.3 %collective-permute-done.5.g2 = bf16[16,128]{1,0:T(8,128)(2,1)S(1)} collective-permute-done((bf16[16,128]{1,0:T(8,128)(2,1)S(1)}, bf16[16,128]{1,0:T(8,128)(2,1)S(1)}, u32[]{:S(2)}, u32[]{:S(2)}) %collective-permute-start.5) | collective-permute-done | bytes 4128 | tf_op jit(solution)/shard_map/ppermute | solution.py:584
  48.4 0.0 collective-permute-done.2.r1
  48.4 0.0 collective-permute-done.3.r2
  48.5 8.6 %step2.1 = f32[3,40,16,640]{3,2,1,0:T(8,128)} custom-call(s32[4]{0:T(128)S(1)} %pad_add_fusion.idx, bf16[5,128,128]{2,1,0:T(8,128)(2,1)S(1)} %collective-permute-done.2.r1, bf16[5,128,128]{2,1,0:T(8,128)(2,1)S(1)} %collective-permute-done.3.r2, bf16[16,128]{1,0:T(8,128)(2,1)S(1)} %collective-permute-done.4.g1, ...), custom_call_target="tpu_custom_call" | custom-call | bytes 21000000 | tf_op jit(solution)/shard_map/step2/pallas_call | solution.py:585
  (7 shorter events, 0.0 us)
Async XLA Ops:
  5.3 23.8 %all-to-all-start = ((bf16[16,8,16,128]{3,2,1,0:T(8,128)(2,1)}), bf16[16,8,16,128]{3,2,1,0:T(8,128)(2,1)S(1)}, u32[]{:S(2)}, u32[]{:S(2)}) async-start(bf16[16,8,16,128]{3,2,1,0:T(8,128)(2,1)} %get-tuple-element.26), calls=%async_computation | async-start | bytes 1048576 | tf_op jit(solution)/shard_map/all_to_all | solution.py:546
  13.2 15.9 %collective-permute-start = (bf16[5,208,128]{2,1,0:T(8,128)(2,1)S(1)}, bf16[5,208,128]{2,1,0:T(8,128)(2,1)S(1)}, u32[]{:S(2)}, u32[]{:S(2)}) collective-permute-start(bf16[5,208,128]{2,1,0:T(8,128)(2,1)S(1)} %get-tuple-element.32), channel_id=1, source_target_pairs={{0,16},{16,0},{32,48},{48,32},{64,80},{80,64},{96,112},{112,96},{1... | collective-permute-start | bytes 798728 | tf_op jit(solution)/shard_map/ppermute | solution.py:544
  13.8 15.3 %copy-start.2 = (s32[16,640]{1,0:T(8,128)S(1)}, s32[16,640]{1,0:T(8,128)}, u32[]{:S(2)}) copy-start(s32[16,640]{1,0:T(8,128)} %wet.3) | copy-start | bytes 122884
  13.8 15.3 %copy-start.3 = (s32[80,4]{0,1:T(4,128)S(1)}, s32[80,4]{0,1:T(4,128)}, u32[]{:S(2)}) copy-start(s32[80,4]{0,1:T(4,128)} %param.17) | copy-start | bytes 3844
  13.8 15.3 %copy-start.4 = (f32[3,10]{1,0:T(4,128)S(1)}, f32[3,10]{1,0:T(4,128)}, u32[]{:S(2)}) copy-start(f32[3,10]{1,0:T(4,128)} %coup.1) | copy-start | bytes 364
  13.8 15.4 %copy-start.5 = (s32[80]{0:T(128)S(1)}, s32[80]{0:T(128)}, u32[]{:S(2)}) copy-start(s32[80]{0:T(128)} %live.1) | copy-start | bytes 964
  13.8 15.3 %collective-permute-start.1 = (bf16[5,208,128]{2,1,0:T(8,128)(2,1)S(1)}, bf16[5,208,128]{2,1,0:T(8,128)(2,1)S(1)}, u32[]{:S(2)}, u32[]{:S(2)}) collective-permute-start(bf16[5,208,128]{2,1,0:T(8,128)(2,1)S(1)} %get-tuple-element.33), channel_id=1, source_target_pairs={{16,32},{48,64},{80,96},{32,16},{64,48},{96,80},{17,33},{49,65},{8... | collective-permute-start | bytes 798728 | tf_op jit(solution)/shard_map/ppermute | solution.py:545
  29.2 19.2 %copy-start = (f32[5,5,40,16,128]{4,3,2,1,0:T(8,128)S(1)}, f32[5,5,40,16,128]{4,3,2,1,0:T(8,128)}, u32[]{:S(2)}) copy-start(f32[5,5,40,16,128]{4,3,2,1,0:T(8,128)} %get-tuple-element.45.coefs) | copy-start | bytes 24576004
  29.2 19.2 %copy-start.1 = (f32[5,3,40,16,128]{4,3,2,1,0:T(8,128)S(1)}, f32[5,3,40,16,128]{4,3,2,1,0:T(8,128)}, u32[]{:S(2)}) copy-start(f32[5,3,40,16,128]{4,3,2,1,0:T(8,128)} %get-tuple-element.46.first_in) | copy-start | bytes 14745604
  36.4 12.0 %collective-permute-start.2 = (bf16[5,128,128]{2,1,0:T(8,128)(2,1)S(1)}, bf16[5,128,128]{2,1,0:T(8,128)(2,1)S(1)}, u32[]{:S(2)}, u32[]{:S(2)}) collective-permute-start(bf16[5,128,128]{2,1,0:T(8,128)(2,1)S(1)} %get-tuple-element.34), channel_id=1, source_target_pairs={{0,16},{16,0},{32,48},{48,32},{64,80},{80,64},{96,112},{112,96},{1... | collective-permute-start | bytes 491528 | tf_op jit(solution)/shard_map/ppermute | solution.py:581
  36.5 11.9 %collective-permute-start.3 = (bf16[5,128,128]{2,1,0:T(8,128)(2,1)S(1)}, bf16[5,128,128]{2,1,0:T(8,128)(2,1)S(1)}, u32[]{:S(2)}, u32[]{:S(2)}) collective-permute-start(bf16[5,128,128]{2,1,0:T(8,128)(2,1)S(1)} %get-tuple-element.35), channel_id=1, source_target_pairs={{16,32},{48,64},{80,96},{32,16},{64,48},{96,80},{17,33},{49,65},{8... | collective-permute-start | bytes 491528 | tf_op jit(solution)/shard_map/ppermute | solution.py:582
  40.9 6.2 %collective-permute-start.4 = (bf16[16,128]{1,0:T(8,128)(2,1)S(1)}, bf16[16,128]{1,0:T(8,128)(2,1)S(1)}, u32[]{:S(2)}, u32[]{:S(2)}) collective-permute-start(bf16[16,128]{1,0:T(8,128)(2,1)S(1)} %get-tuple-element.36), channel_id=1, source_target_pairs={{0,1},{1,0},{2,3},{3,2},{4,5},{5,4},{6,7},{7,6},{8,9},{9,8},{10,11... | collective-permute-start | bytes 12296 | tf_op jit(solution)/shard_map/ppermute | solution.py:583
  41.0 7.4 %collective-permute-start.5 = (bf16[16,128]{1,0:T(8,128)(2,1)S(1)}, bf16[16,128]{1,0:T(8,128)(2,1)S(1)}, u32[]{:S(2)}, u32[]{:S(2)}) collective-permute-start(bf16[16,128]{1,0:T(8,128)(2,1)S(1)} %get-tuple-element.37), channel_id=1, source_target_pairs={{1,2},{3,4},{5,6},{7,8},{9,10},{11,12},{13,14},{15,0},{2,1},{4,3},... | collective-permute-start | bytes 12296 | tf_op jit(solution)/shard_map/ppermute | solution.py:584
